TPU v7x, 256 devices: a whole 4x4x8 slice. The times are simulated.
256 devices in a mesh: layer: 8 (over y_lo, x), prow: 4 (over y_hi, core), pcol: 8 (over z).
Axes of the slice: x: 4, y: 4 (y_hi: 2, y_lo: 2; y = y_hi * 2 + y_lo), z: 8, core: 2. Of those that a mesh axis runs over, the one named last changes fastest.
Arguments:
- front_blocks: float32 [8, 4, 1024, 4, 1024], P('layer', None, 'prow', None, 'pcol'), may hold values from -6 to 6, as said below
- fill_mask: int32 [32, 32], replicated, may hold values from 0 to 1, as said below
Outputs:
- factored: float32 [8, 4, 1024, 4, 1024], P('layer', None, 'prow', None, 'pcol')
- ancestor: float32 [3, 4, 8, 32, 3, 1024], P(None, 'prow', 'layer', None, None, 'pcol')
Inputs may be any that keep to these rules, and one draw needn't show every extreme that they name: `front_blocks`: with the fill pattern applied, every pivot block that the elimination meets is invertible and well conditioned. `fill_mask`: block row i is filled exactly from some block column at most i // 2 through the diagonal block, and block column j exactly from some block row at most j // 2 through the diagonal block; all other block pairs are empty.
All inputs are finite; a program needn't handle non-finite values.
Results may differ from a plain program's by a relative error of at most 0.0001.
Values sent between devices are 32-bit elements; how exact they have to be, the bound alone decides.
A program may use at most 128 MiB of HBM per device.

v0:
```python
import jax
import jax.numpy as jnp
from jax import lax
from jax.sharding import Mesh
from jax.sharding import PartitionSpec as P

P_SIZE = 1024
BS = 128
PANELS = 1
PROW = ("prow_0", "prow_1")
PROW_PCOL = ("prow_0", "prow_1", "pcol")


def edges_of(length, count):
    lap = length // count
    if lap >= 8:
        lap -= lap % 8
    return [lap * k for k in range(1, count)]


def all_blocks(shard, axes, order):
    tiles = shard[None]
    for k in order:
        tiles = lax.all_gather(tiles, axes[k], axis=0, tiled=True)
    block = [lax.axis_size(axes[k]) for k in reversed(order)]
    tiles = tiles.reshape(*block, *shard.shape)
    turned = sorted(range(len(order)), key=lambda place: order[len(order) - 1 - place])
    return tiles.transpose(*turned, *range(len(order), tiles.ndim)).reshape(-1, *shard.shape)


def joined_along(tiles, dim):
    tiles = jnp.moveaxis(tiles, 0, dim)
    shape = tiles.shape
    return tiles.reshape(*shape[:dim], shape[dim] * shape[dim + 1], *shape[dim + 2 :])


def gather_all_axes(shard, axes, dim):
    numbers = list(range(len(axes)))[::-1]
    widest = shard.shape.index(max(shard.shape[:-1] or shard.shape))
    edges = [0, *edges_of(shard.shape[widest], len(axes)), shard.shape[widest]]
    finished = []
    for k, (start, end) in enumerate(zip(edges, edges[1:])):
        if end > start:
            share = lax.slice_in_dim(shard, start, end, axis=widest)
            finished.append(all_blocks(share, axes, numbers[k:] + numbers[:k]))
    return joined_along(jnp.concatenate(finished, axis=widest + 1), dim)


def sent_to_all(shard, axis):
    copies = jnp.broadcast_to(shard, (lax.axis_size(axis), *shard.shape))
    return lax.all_to_all(copies, axis, split_axis=0, concat_axis=0, tiled=True)


def gathered_copies(shard, axis, dim):
    tiles = sent_to_all(shard, axis)
    return joined_along(tiles, dim)


def cut_along(shard, dim, length):
    shape = shard.shape
    tiles = shard.reshape(*shape[:dim], length, shape[dim] // length, *shape[dim + 1 :])
    return jnp.moveaxis(tiles, dim, 0)


def summed_on_arrival(shard, axis, dim):
    length = lax.axis_size(axis)
    tiles = lax.all_to_all(cut_along(shard, dim, length), axis, 0, 0, tiled=True)
    return jnp.sum(tiles, axis=0)


def full_dot(left, right):
    return jnp.dot(left, right, precision=lax.Precision.HIGHEST, preferred_element_type=jnp.float32)


def invert(pivot_tile):
    gram_matrix = full_dot(pivot_tile.T, pivot_tile)
    cholesky_factor = jnp.linalg.cholesky(gram_matrix)
    return jax.scipy.linalg.cho_solve((cholesky_factor, True), pivot_tile.T)


def factor_pivot(matrix):
    pieces = []
    remainder = matrix
    for position in range(matrix.shape[0] // BS):
        pivot_tile = remainder[:BS, :BS]
        inverse = invert(pivot_tile)
        lower_part = full_dot(remainder[BS:, :BS], inverse)
        upper_part = remainder[:BS, BS:]
        pieces.append((pivot_tile, inverse, lower_part, upper_part))
        remainder = remainder[BS:, BS:] - full_dot(lower_part, upper_part)
    return pieces


def assemble(pieces):
    columns_list = []
    for column, piece in enumerate(pieces):
        above_part = [
            pieces[earlier][3][:, (column - earlier - 1) * BS : (column - earlier) * BS]
            for earlier in range(column)
        ]
        columns_list.append(jnp.concatenate(above_part + [piece[0], piece[2]], axis=0))
    return jnp.concatenate(columns_list, axis=1)


def solve_lower(row_data, pieces):
    results = []
    remaining_cols = row_data
    for pivot_tile, inverse, lower_part, upper_part in pieces:
        solved = full_dot(remaining_cols[:, :BS], inverse)
        results.append(solved)
        remaining_cols = remaining_cols[:, BS:] - full_dot(solved, upper_part)
    return jnp.concatenate(results, axis=1)


def solve_upper(column_data, pieces):
    results = []
    remaining_rows = column_data
    for pivot_tile, inverse, lower_part, upper_part in pieces:
        leading = remaining_rows[:BS]
        results.append(leading)
        remaining_rows = remaining_rows[BS:] - full_dot(lower_part, leading)
    return jnp.concatenate(results, axis=0)


def on_device(front_blocks, fill_mask):
    grid_row = lax.axis_index(PROW)
    grid_col = lax.axis_index("pcol")
    row_groups = lax.axis_size(PROW)
    col_groups = lax.axis_size("pcol")
    supers = front_blocks.shape[1]
    rows_dev = front_blocks.shape[2]
    cols_dev = front_blocks.shape[4]
    blocks_row = rows_dev // BS
    blocks_col = cols_dev // BS
    fill_table = fill_mask.reshape(supers, P_SIZE // BS, supers, P_SIZE // BS)
    fill_table = lax.dynamic_slice(
        fill_table,
        (0, grid_row * blocks_row, 0, grid_col * blocks_col),
        (supers, blocks_row, supers, blocks_col),
    )
    fill_table = jnp.broadcast_to(
        fill_table[:, :, None, :, :, None], (supers, blocks_row, BS, supers, blocks_col, BS)
    )
    fill_table = fill_table.reshape(supers, rows_dev, supers, cols_dev).astype(jnp.float32)
    current = front_blocks[0] * fill_table
    remaining = supers - 1
    own_tile = current[0, :, 0, :]
    gathered = gather_all_axes(own_tile[None], PROW_PCOL, 0)
    pivot_full = (
        gathered.reshape(row_groups, col_groups, rows_dev, cols_dev)
        .transpose(0, 2, 1, 3)
        .reshape(P_SIZE, P_SIZE)
    )
    pieces = factor_pivot(pivot_full)
    upper_rows = gathered_copies(current[0, :, 1:, :], PROW, 0)
    solved_upper = solve_upper(upper_rows.reshape(P_SIZE, remaining * cols_dev), pieces)
    below_part = current[1:, :, 0, :]
    widened = lax.all_gather(below_part, "pcol", axis=2, tiled=True)
    lower_rows = solve_lower(widened.reshape(remaining * rows_dev, P_SIZE), pieces).reshape(
        remaining, rows_dev, P_SIZE
    )
    factored_pivot = assemble(pieces)
    own_pivot = lax.dynamic_slice(
        factored_pivot, (grid_row * rows_dev, grid_col * cols_dev), (rows_dev, cols_dev)
    )
    own_upper = lax.dynamic_slice_in_dim(solved_upper, grid_row * rows_dev, rows_dev, 0).reshape(
        rows_dev, remaining, cols_dev
    )
    own_lower = lax.dynamic_slice_in_dim(lower_rows, grid_col * cols_dev, cols_dev, 2)
    update_term = full_dot(lower_rows.reshape(remaining * rows_dev, P_SIZE), solved_upper)
    trailing = current[1:, :, 1:, :] - update_term.reshape(remaining, rows_dev, remaining, cols_dev)
    current = current.at[0, :, 0, :].set(own_pivot)
    current = current.at[0, :, 1:, :].set(own_upper)
    current = current.at[1:, :, 0, :].set(own_lower)
    current = current.at[1:, :, 1:, :].set(trailing)
    trailing_own = current[PANELS:, :, PANELS:, :]
    summed = summed_on_arrival(trailing_own, "layer", 1)
    ancestor_rows = summed.shape[1]
    ancestor_part = summed.reshape(supers - PANELS, 1, 1, ancestor_rows, supers - PANELS, cols_dev)
    return (current[None], ancestor_part)


def solution(mesh):
    torus = Mesh(
        mesh.devices.reshape(mesh.shape["layer"], 2, 2, mesh.shape["pcol"]),
        ("layer", "prow_0", "prow_1", "pcol"),
    )
    placed = (P("layer", None, PROW, None, "pcol"), P())
    return jax.shard_map(
        on_device,
        mesh=torus,
        in_specs=placed,
        out_specs=(
            P("layer", None, PROW, None, "pcol"),
            P(None, PROW, "layer", None, None, "pcol"),
        ),
        check_vma=False,
    )
```

profile of v0, /device:TPU:1, one launch (start us, length us, event | category | flops | bytes accessed | tf_op | source)
XLA Modules:
  0.0 524.0 jit_solution(7103626663641285439)
XLA Ops:
  7.2 2.9 copy.63
  12.7 23.4 %all-gather = f32[8,80,128]{2,1,0:T(8,128)S(1)} all-gather(f32[1,80,128]{2,1,0:T(8,128)S(1)} %copy.66), channel_id=2, replica_groups=mesh['layer'=8,'prow_0'=2,'prow_1'=2,'pcol'=8] {'pcol'}, dimensions={0}, use_global_device_ids=true | all-gather | bytes 368640 | tf_op jit(solution)/shard_map/all_gather | solution.py:24
  36.1 8.8 %all-gather.1 = f32[16,80,128]{2,1,0:T(8,128)} all-gather(f32[8,80,128]{2,1,0:T(8,128)S(1)} %all-gather), channel_id=3, replica_groups=mesh['layer'=8,'prow_0'=2,'prow_1'=2,'pcol'=8] {'prow_1'}, dimensions={0}, use_global_device_ids=true | all-gather | bytes 983040 | tf_op jit(solution)/shard_map/all_gather | solution.py:24
  45.2 5.1 all-gather.6
  50.3 23.7 %all-gather.7 = f32[16,96,128]{2,1,0:T(8,128)} all-gather(f32[2,96,128]{2,1,0:T(8,128)S(1)} %all-gather.6), channel_id=9, replica_groups=mesh['layer'=8,'prow_0'=2,'prow_1'=2,'pcol'=8] {'pcol'}, dimensions={0}, use_global_device_ids=true | all-gather | bytes 884736 | tf_op jit(solution)/shard_map/all_gather | solution.py:24
  74.2 7.4 %all-gather.3 = f32[2,80,128]{2,1,0:T(8,128)S(1)} all-gather(f32[1,80,128]{2,1,0:T(8,128)S(1)} %copy.67), channel_id=5, replica_groups=mesh['layer'=8,'prow_0'=2,'prow_1'=2,'pcol'=8] {'prow_1'}, dimensions={0}, use_global_device_ids=true | all-gather | bytes 122880 | tf_op jit(solution)/shard_map/all_gather | solution.py:24
  81.6 5.9 %all-gather.4 = f32[4,80,128]{2,1,0:T(8,128)} all-gather(f32[2,80,128]{2,1,0:T(8,128)S(1)} %all-gather.3), channel_id=6, replica_groups=mesh['layer'=8,'prow_0'=2,'prow_1'=2,'pcol'=8] {'prow_0'}, dimensions={0}, use_global_device_ids=true | all-gather | bytes 245760 | tf_op jit(solution)/shard_map/all_gather | solution.py:24
  88.8 5.7 %all-to-all-start = ((f32[4,256,3,128]{1,3,2,0:T(8,128)}), f32[4,256,3,128]{1,3,2,0:T(8,128)}, u32[]{:S(2)}, u32[]{:S(2)}) async-start(f32[4,256,3,128]{1,3,2,0:T(8,128)} %broadcast_in_dim.36), calls=%async_computation | async-start | bytes 3145728 | tf_op jit(solution)/shard_map/all_to_all | solution.py:51
  97.3 17.9 %all-to-all-done = f32[4,256,3,128]{1,3,2,0:T(8,128)} async-done(((f32[4,256,3,128]{1,3,2,0:T(8,128)}), f32[4,256,3,128]{1,3,2,0:T(8,128)}, u32[]{:S(2)}, u32[]{:S(2)}) %all-to-all-start) | async-done | bytes 1572896 | tf_op jit(solution)/shard_map/all_to_all | solution.py:51
  115.2 2.1 copy.92
  121.1 2.3 copy.70
  123.4 8.8 %all-gather.17.cloned.1.call-done = f32[32,80,128]{2,1,0:T(8,128)} async-done(((f32[4,80,128]{2,1,0:T(8,128)}), f32[32,80,128]{2,1,0:T(8,128)}) %all-gather.17.cloned.1.call-update) | async-done | bytes 1310736 | tf_op jit(solution)/shard_map/all_gather | solution.py:24
  132.2 2.1 copy.68
  137.9 11.7 %cholesky.134 = f32[128,128]{1,0:T(8,128)S(1)} custom-call(f32[128,128]{1,0:T(8,128)S(1)} %fusion.103), custom_call_target="Cholesky" | custom-call | tf_op jit(solution)/shard_map/jit(cholesky)/cholesky | solution.py:77
  151.0 9.8 %custom-call.14 = f32[1,128,128]{1,2,0:T(8,128)S(1)} custom-call(f32[1,128,128]{2,1,0:T(8,128)S(1)} %fusion.46), custom_call_target="InvertDiagBlocksLowerTriangular" | custom-call | tf_op jit(solution)/shard_map/jit(_cho_solve)/triangular_solve | solution.py:78
  165.1 5.2 slice_subtract_fusion
  172.6 11.7 %cholesky.145 = f32[128,128]{1,0:T(8,128)S(1)} custom-call(f32[128,128]{1,0:T(8,128)S(1)} %fusion.97), custom_call_target="Cholesky" | custom-call | tf_op jit(solution)/shard_map/jit(cholesky)/cholesky | solution.py:77
  185.7 9.8 %custom-call.15 = f32[1,128,128]{1,2,0:T(8,128)S(1)} custom-call(f32[1,128,128]{2,1,0:T(8,128)S(1)} %fusion.47), custom_call_target="InvertDiagBlocksLowerTriangular" | custom-call | tf_op jit(solution)/shard_map/jit(_cho_solve)/triangular_solve | solution.py:78
  202.2 11.9 %cholesky.156 = f32[128,128]{1,0:T(8,128)S(1)} custom-call(f32[128,128]{1,0:T(8,128)S(1)} %fusion.91), custom_call_target="Cholesky" | custom-call | tf_op jit(solution)/shard_map/jit(cholesky)/cholesky | solution.py:77
  215.5 9.8 %custom-call.16 = f32[1,128,128]{1,2,0:T(8,128)S(1)} custom-call(f32[1,128,128]{2,1,0:T(8,128)S(1)} %fusion.48), custom_call_target="InvertDiagBlocksLowerTriangular" | custom-call | tf_op jit(solution)/shard_map/jit(_cho_solve)/triangular_solve | solution.py:78
  228.7 3.0 slice_subtract_fusion.5
  243.6 13.2 %cholesky.167 = f32[128,128]{1,0:T(8,128)} custom-call(f32[128,128]{1,0:T(8,128)} %fusion.85), custom_call_target="Cholesky" | custom-call | tf_op jit(solution)/shard_map/jit(cholesky)/cholesky | solution.py:77
  258.3 2.2 fusion.49
  260.5 11.4 %custom-call.17 = f32[1,128,128]{1,2,0:T(8,128)} custom-call(f32[1,128,128]{2,1,0:T(8,128)} %fusion.49), custom_call_target="InvertDiagBlocksLowerTriangular" | custom-call | tf_op jit(solution)/shard_map/jit(_cho_solve)/triangular_solve | solution.py:78
  274.2 2.1 constant_dynamic-update-slice_fusion.10
  281.4 2.3 convolution_subtract_fusion.3
  288.4 13.2 %cholesky.178 = f32[128,128]{1,0:T(8,128)} custom-call(f32[128,128]{1,0:T(8,128)} %fusion.79), custom_call_target="Cholesky" | custom-call | tf_op jit(solution)/shard_map/jit(cholesky)/cholesky | solution.py:77
  303.1 2.1 fusion.50
  305.2 11.3 %custom-call.18 = f32[1,128,128]{1,2,0:T(8,128)} custom-call(f32[1,128,128]{2,1,0:T(8,128)} %fusion.50), custom_call_target="InvertDiagBlocksLowerTriangular" | custom-call | tf_op jit(solution)/shard_map/jit(_cho_solve)/triangular_solve | solution.py:78
  330.2 12.1 %cholesky.189 = f32[128,128]{1,0:T(8,128)S(1)} custom-call(f32[128,128]{1,0:T(8,128)S(1)} %fusion.73), custom_call_target="Cholesky" | custom-call | tf_op jit(solution)/shard_map/jit(cholesky)/cholesky | solution.py:77
  343.6 9.8 %custom-call.19 = f32[1,128,128]{1,2,0:T(8,128)S(1)} custom-call(f32[1,128,128]{2,1,0:T(8,128)S(1)} %fusion.51), custom_call_target="InvertDiagBlocksLowerTriangular" | custom-call | tf_op jit(solution)/shard_map/jit(_cho_solve)/triangular_solve | solution.py:78
  366.5 12.5 %cholesky.200 = f32[128,128]{1,0:T(8,128)S(1)} custom-call(f32[128,128]{1,0:T(8,128)} %fusion.67), custom_call_target="Cholesky" | custom-call | tf_op jit(solution)/shard_map/jit(cholesky)/cholesky | solution.py:77
  381.1 10.6 %custom-call.20 = f32[1,128,128]{1,2,0:T(8,128)S(1)} custom-call(f32[1,128,128]{2,1,0:T(8,128)} %fusion.52), custom_call_target="InvertDiagBlocksLowerTriangular" | custom-call | tf_op jit(solution)/shard_map/jit(_cho_solve)/triangular_solve | solution.py:78
  411.6 2.7 convolution_subtract_fusion
  420.5 11.7 %cholesky.211 = f32[128,128]{1,0:T(8,128)S(1)} custom-call(f32[128,128]{1,0:T(8,128)S(1)} %fusion.61), custom_call_target="Cholesky" | custom-call | tf_op jit(solution)/shard_map/jit(cholesky)/cholesky | solution.py:77
  433.6 10.0 %custom-call.21 = f32[1,128,128]{1,2,0:T(8,128)S(1)} custom-call(f32[1,128,128]{2,1,0:T(8,128)S(1)} %fusion.53), custom_call_target="InvertDiagBlocksLowerTriangular" | custom-call | tf_op jit(solution)/shard_map/jit(_cho_solve)/triangular_solve | solution.py:78
  444.1 2.1 bitcast_dynamic-update-slice_fusion.2
  446.1 3.5 copy.84
  451.2 4.5 slice_subtract_fusion.1
  456.2 3.2 slice_subtract_fusion.2
  460.0 2.8 slice_subtract_fusion.4
  463.4 2.4 slice_subtract_fusion.6
  466.4 2.1 convolution_subtract_fusion.1
  473.7 2.4 copy.86
  476.1 7.5 %fusion.131 = f32[768,384]{1,0:T(8,128)} fusion(f32[768,1024]{0,1:T(8,128)S(1)} %convolution_dynamic-update-slice_fusion, f32[1024,384]{1,0:T(8,128)} %copy-done.16), kind=kOutput, calls=%fused_computation.254 | convolution fusion | flops 3623878656 | bytes 5898240 | tf_op jit(solution)/shard_map/dot_general | solution.py:72
  485.6 2.9 reshape.233
  496.5 4.9 all-to-all-start.1
  503.2 13.1 %all-to-all-done.1 = f32[8,3,32,3,128]{4,2,3,1,0:T(8,128)S(1)} async-done(((f32[8,3,32,3,128]{4,2,3,1,0:T(8,128)}), f32[8,3,32,3,128]{4,2,3,1,0:T(8,128)S(1)}, u32[]{:S(2)}, u32[]{:S(2)}) %all-to-all-start.1) | async-done | bytes 1179680 | tf_op jit(solution)/shard_map/all_to_all | solution.py:67
  (271 shorter events, 140.8 us)
Async XLA Ops:
  7.2 3.0 copy-start.44
  7.2 112.1 %all-gather.15.cloned.1.call-start = ((), (), s32[]{:S(2)}) async-start(), calls=%async_computation.2 | async-start | bytes 1966080 | tf_op jit(solution)/shard_map/all_gather | solution.py:24
  12.5 82.8 %copy-start = (f32[4,256,4,128]{1,3,2,0:T(8,128)}, f32[4,256,4,128]{1,3,2,0:T(8,128)S(1)}, u32[]{:S(2)}) copy-start(f32[4,256,4,128]{1,3,2,0:T(8,128)S(1)} %bitcast_multiply_fusion) | copy-start | bytes 6291460
  45.0 76.1 %all-gather.19.cloned.1.call-start = ((), (), s32[]{:S(2)}) async-start(), calls=%async_computation.4 | async-start | bytes 2359296 | tf_op jit(solution)/shard_map/all_gather | solution.py:24
  74.0 58.2 %all-gather.17.cloned.1.call-start = ((), (), s32[]{:S(2)}) async-start(), calls=%async_computation.3 | async-start | bytes 1474560 | tf_op jit(solution)/shard_map/all_gather | solution.py:24
  88.8 26.4 %all-to-all-start = ((f32[4,256,3,128]{1,3,2,0:T(8,128)}), f32[4,256,3,128]{1,3,2,0:T(8,128)}, u32[]{:S(2)}, u32[]{:S(2)}) async-start(f32[4,256,3,128]{1,3,2,0:T(8,128)} %broadcast_in_dim.36), calls=%async_computation | async-start | bytes 3145728 | tf_op jit(solution)/shard_map/all_to_all | solution.py:51
  94.5 1.4 copy-start.45
  94.5 351.6 %all-gather.21.cloned.1.call-start = ((), (), s32[]{:S(2)}) async-start(), calls=%async_computation.5 | async-start | bytes 3538944 | tf_op jit(solution)/shard_map/all_gather | solution.py:158
  117.5 1.1 copy-start.18
  135.6 1.9 copy-start.3
  164.3 0.8 copy-start.6
  170.3 151.9 %copy-start.5 = (f32[896,896]{1,0:T(8,128)}, f32[896,896]{1,0:T(8,128)S(1)}, u32[]{:S(2)}) copy-start(f32[896,896]{1,0:T(8,128)S(1)} %slice_subtract_fusion) | copy-start | bytes 9633796
  195.5 5.8 %copy-start.7 = (f32[896,128]{1,0:T(8,128)S(1)}, f32[896,128]{1,0:T(8,128)}, u32[]{:S(2)}) copy-start(f32[896,128]{1,0:T(8,128)} %copy-done.6) | copy-start | bytes 1376260
  197.1 4.2 copy-start.10
  199.1 1.5 copy-start.9
  225.3 6.4 %copy-start.11 = (f32[768,128]{1,0:T(8,128)S(1)}, f32[768,128]{1,0:T(8,128)}, u32[]{:S(2)}) copy-start(f32[768,128]{1,0:T(8,128)} %copy-done.10) | copy-start | bytes 1179652
  225.3 8.3 %copy-start.43 = (f32[128,128]{1,0:T(8,128)S(1)}, f32[128,128]{1,0:T(8,128)}, u32[]{:S(2)}) copy-start(f32[128,128]{1,0:T(8,128)} %slice.541) | copy-start | bytes 196612
  231.7 8.2 %copy-start.13 = (f32[640,640]{1,0:T(8,128)}, f32[640,640]{1,0:T(8,128)S(1)}, u32[]{:S(2)}) copy-start(f32[640,640]{1,0:T(8,128)S(1)} %slice_subtract_fusion.5) | copy-start | bytes 4915204
  274.2 7.2 %copy-start.36 = (f32[128,128]{1,0:T(8,128)}, f32[128,128]{1,0:T(8,128)S(1)}, u32[]{:S(2)}) copy-start(f32[128,128]{1,0:T(8,128)S(1)} %fusion.82) | copy-start | bytes 196612
  276.3 5.1 copy-start.19
  283.7 1.0 copy-start.14
  318.7 8.6 %copy-start.26 = (f32[128,128]{1,0:T(8,128)}, f32[128,128]{1,0:T(8,128)S(1)}, u32[]{:S(2)}) copy-start(f32[128,128]{1,0:T(8,128)S(1)} %fusion.76) | copy-start | bytes 196612
  320.7 6.6 %copy-start.22 = (f32[384,128]{1,0:T(8,128)}, f32[384,128]{1,0:T(8,128)S(1)}, u32[]{:S(2)}) copy-start(f32[384,128]{1,0:T(8,128)S(1)} %get-tuple-element.70) | copy-start | bytes 589828
  329.1 81.1 %copy-start.17 = (f32[384,384]{1,0:T(8,128)}, f32[384,384]{1,0:T(8,128)S(1)}, u32[]{:S(2)}) copy-start(f32[384,384]{1,0:T(8,128)S(1)} %convolution_subtract_fusion.8) | copy-start | bytes 1769476
  329.1 80.2 %copy-start.2 = (f32[4,256,4,128]{1,3,2,0:T(8,128)S(1)}, f32[4,256,4,128]{1,3,2,0:T(8,128)}, u32[]{:S(2)}) copy-start(f32[4,256,4,128]{1,3,2,0:T(8,128)} %copy-done) | copy-start | bytes 6291460
  353.9 40.0 %copy-start.28 = (f32[128,128]{1,0:T(8,128)}, f32[128,128]{1,0:T(8,128)S(1)}, u32[]{:S(2)}) copy-start(f32[128,128]{1,0:T(8,128)S(1)} %fusion.70) | copy-start | bytes 196612
  354.9 39.0 %copy-start.24 = (f32[256,128]{1,0:T(8,128)}, f32[256,128]{1,0:T(8,128)S(1)}, u32[]{:S(2)}) copy-start(f32[256,128]{1,0:T(8,128)S(1)} %get-tuple-element.72) | copy-start | bytes 393220
  363.3 30.6 %copy-start.21 = (f32[256,256]{1,0:T(8,128)}, f32[256,256]{1,0:T(8,128)S(1)}, u32[]{:S(2)}) copy-start(f32[256,256]{1,0:T(8,128)S(1)} %convolution_subtract_fusion.11) | copy-start | bytes 786436
  393.9 10.4 %copy-start.30 = (f32[128,128]{1,0:T(8,128)}, f32[128,128]{1,0:T(8,128)S(1)}, u32[]{:S(2)}) copy-start(f32[128,128]{1,0:T(8,128)S(1)} %fusion.64) | copy-start | bytes 196612
  394.8 9.6 %copy-start.38 = (f32[128,128]{1,0:T(8,128)}, f32[128,128]{1,0:T(8,128)S(1)}, u32[]{:S(2)}) copy-start(f32[128,128]{1,0:T(8,128)S(1)} %get-tuple-element.74) | copy-start | bytes 196612
  394.8 16.8 %copy-start.8 = (f32[896,128]{1,0:T(8,128)S(1)}, f32[896,128]{1,0:T(8,128)}, u32[]{:S(2)}) copy-start(f32[896,128]{1,0:T(8,128)} %copy-done.6) | copy-start | bytes 1376260
  410.2 4.1 copy-start.15
  410.2 4.1 copy-start.12
  411.6 4.9 copy-start.20
  414.3 2.9 copy-start.23
  414.4 3.5 copy-start.25
  415.5 3.0 copy-start.39
  418.7 1.2 copy-start.16
  446.1 3.6 copy-start.41
  451.2 4.5 copy-start.33
  455.7 3.7 copy-start.35
  459.4 3.4 copy-start.37
  462.8 3.0 copy-start.27
  463.4 5.1 copy-start.29
  466.3 4.7 copy-start.31
  485.6 6.3 %copy-start.1 = (f32[4,256,4,128]{1,3,2,0:T(8,128)S(1)}, f32[4,256,4,128]{1,3,2,0:T(8,128)}, u32[]{:S(2)}) copy-start(f32[4,256,4,128]{1,3,2,0:T(8,128)} %copy-done) | copy-start | bytes 6291460
  493.6 7.8 %copy-start.4 = (f32[1,4,256,4,128]{2,4,3,1,0:T(8,128)S(1)}, f32[1,4,256,4,128]{2,4,3,1,0:T(8,128)}, u32[]{:S(2)}) copy-start(f32[1,4,256,4,128]{2,4,3,1,0:T(8,128)} %get-tuple-element.58) | copy-start | bytes 6291460
  496.5 19.8 %all-to-all-start.1 = ((f32[8,3,32,3,128]{4,2,3,1,0:T(8,128)}), f32[8,3,32,3,128]{4,2,3,1,0:T(8,128)S(1)}, u32[]{:S(2)}, u32[]{:S(2)}) async-start(f32[8,3,32,3,128]{4,2,3,1,0:T(8,128)} %copy.90), calls=%async_computation.1 | async-start | bytes 2359296 | tf_op jit(solution)/shard_map/all_to_all | solution.py:67
  (4 other events, 2.5 us)
Sparse Core Ops, SparseCore 0:
  45.1 29.5 all-gather.14
  76.4 17.9 all-gather.18
  96.2 35.9 all-gather.16
  133.9 47.1 all-gather.20
where the time goes:
time: 531 us; the launch traced here: 524 us
  other arithmetic  214 us (40%)
  local copies, waits for them, and re-layouts  92.3 us (17%)
  matrix products  77.4 us (15%)
  blocking collectives  74.4 us (14%)
  waiting for transfers between devices  39.9 us (8%)
  between operations  15.5 us (3%)
  starting transfers between devices  10.7 us (2%)
    another operation x24, other arithmetic, invert(): cholesky_factor = jnp.linalg.cholesky(gram_matrix)  105 us
    another operation x16, other arithmetic, invert(): return jax.scipy.linalg.cho_solve((cholesky_factor, True), pivot_tile.T)  91.4 us
    all_gather x6, blocking collectives, all_blocks(): tiles = lax.all_gather(tiles, axes[k], axis=0, tiled=True)  74.4 us
    dot_general x45, matrix products, full_dot(): jnp.dot(left, right, precision=lax.Precision.HIGHEST, preferred_element_t...  67.3 us
    unnamed x134, local copies, waits for them, and re-layouts  52.4 us
    all_to_all x1, waiting for transfers between devices, sent_to_all(): return lax.all_to_all(copies, axis, split_axis=0, concat_axis=0, tiled=True)  17.9 us
    all_to_all x1, waiting for transfers between devices, summed_on_arrival(): lax.all_to_all(cut_along(shard, dim, length), axis, 0, 0, tiled=True)  13.1 us
  transfers between devices with their start and end apart: 6, of which 3 were waited for; matrix products, arithmetic and copies ran while one was open for 61% of the time, Pallas kernels for 0%

commit v1 on v0

v1 whole, which is shorter than its diff:
```python
import jax
import jax.numpy as jnp
from jax import lax
from jax.experimental import pallas as pl
from jax.experimental.pallas import tpu as pltpu
from jax.sharding import PartitionSpec as P

BS = 128
MESH = pl.DeviceIdType.MESH


def dot(left, right, dims=((1,), (0,)), precision=lax.Precision.HIGHEST):
    return lax.dot_general(
        left, right, (dims, ((), ())), precision=precision, preferred_element_type=jnp.float32
    )


def bulk(left, right):
    return dot(left, right, precision=lax.Precision.HIGH)


def lanes_of(block, column):
    return jnp.broadcast_to(block[:, column : column + 1], (8, BS))


def row_of(block, row):
    return jnp.broadcast_to(block[row : row + 1, :], (8, BS))


def invert(pivot, unit_ref, scaled_ref):
    gram = dot(pivot, pivot, ((1,), (1,)))
    groups = [gram[8 * p : 8 * p + 8, :] for p in range(BS // 8)]
    lane = lax.broadcasted_iota(jnp.int32, (8, BS), 1)
    sub = lax.broadcasted_iota(jnp.int32, (8, BS), 0)
    for p in range(BS // 8):
        rows = groups[p]
        own = (lane >= 8 * p) & (lane < 8 * p + 8)
        eye = jnp.where(lane - 8 * p == sub, 1.0, 0.0)
        columns = [lanes_of(rows, 8 * p + j) for j in range(8)]
        unit_ref[8 * p : 8 * p + 8, :] = jnp.where(lane < 8 * p, rows, eye)
        rows = jnp.where(own, eye, rows)
        for k in range(8):
            at = sub == k
            factor = columns[k]
            scale = 1.0 / row_of(factor, k)
            top = row_of(rows, k)
            rows = jnp.where(at, top * scale, rows - (factor * top) * scale)
            for j in range(k + 1, 8):
                top = row_of(columns[j], k)
                columns[j] = jnp.where(at, top * scale, columns[j] - (factor * top) * scale)
        scaled_ref[8 * p : 8 * p + 8, :] = jnp.where(lane < 8 * p + 8, rows, 0.0)
        tops = [row_of(rows, k) for k in range(8)]
        for q in range(p + 1, BS // 8):
            term = [lanes_of(groups[q], 8 * p + k) * tops[k] for k in range(8)]
            total = ((term[0] + term[1]) + (term[2] + term[3])) + ((term[4] + term[5]) + (term[6] + term[7]))
            groups[q] = jnp.where(own, 0.0, groups[q]) - total
    right = dot(unit_ref[...], pivot)
    return dot(right, scaled_ref[...], ((0,), (0,)))


def kernel(
    x_ref, mask_ref, out_ref, anc_ref,
    praw, uraw, lraw, work, low, tail, got, inv, unit, scaled,
    send, recv, near, far, up_send, up_recv, lo_send, lo_recv, sum_send, sum_recv, local,
):
    layer, row, col = lax.axis_index("layer"), lax.axis_index("prow"), lax.axis_index("pcol")
    cols, rows_n, layers = 8, 4, 8
    mate = row + 1 - 2 * lax.rem(row, 2)
    over = lax.rem(row + 2, rows_n)
    right, left = lax.rem(col + 1, cols), lax.rem(col + cols - 1, cols)

    own = [
        pltpu.make_async_copy(x_ref.at[0, pl.ds(0, 256), :], praw.at[row, col], local.at[0]),
        pltpu.make_async_copy(x_ref.at[0, pl.ds(256, 768), :], lraw.at[col], local.at[1]),
        pltpu.make_async_copy(x_ref.at[pl.ds(1, 3), pl.ds(0, 256), :], uraw.at[row], local.at[2]),
    ]
    for copy in own:
        copy.start()

    barrier = pltpu.get_barrier_semaphore()

    def greet(*device):
        pl.semaphore_signal(barrier, inc=1, device_id=device, device_id_type=MESH)

    greet(layer, mate, col)
    greet(layer, over, col)
    greet(layer, row, right)
    greet(layer, row, left)
    for d in range(1, layers):
        greet(lax.rem(layer + d, layers), row, col)
    pl.semaphore_wait(barrier, 4 + layers - 1)

    def remote(src, dst, send_sem, recv_sem, *device):
        return pltpu.make_async_remote_copy(
            src_ref=src, dst_ref=dst, send_sem=send_sem, recv_sem=recv_sem,
            device_id=device, device_id_type=MESH,
        )

    sent = []

    def go(copy):
        copy.start()
        sent.append(copy)

    groups = (row, over)
    limit = ((4, 3), (3, 4))
    tile = x_ref.at[0, pl.ds(0, 256), :]
    step_to = (right, left)

    def origin(way, hop):
        return lax.rem(col + (cols - hop if way == 0 else hop), cols)

    go(remote(tile, praw.at[row, col], near.at[0], near.at[1], layer, over, col))
    for way in range(2):
        go(remote(tile, praw.at[row, col], send.at[0, way, 0], recv.at[0, way, 0], layer, row, step_to[way]))
    go(remote(tile, praw.at[row, col], near.at[2], near.at[3], layer, mate, col))
    blocks = x_ref.at[pl.ds(1, 3), pl.ds(0, 256), :]
    go(remote(blocks, uraw.at[row], up_send.at[0], up_recv.at[0], layer, over, col))
    go(remote(blocks, uraw.at[row], up_send.at[1], up_recv.at[1], layer, mate, col))
    for copy in own:
        copy.wait()

    place = praw.at[over, col]
    remote(place, place, near.at[0], near.at[1], layer, over, col).wait_recv()
    for way in range(2):
        go(remote(place, place, send.at[1, way, 0], recv.at[1, way, 0], layer, row, step_to[way]))
    go(remote(place, place, near.at[4], near.at[5], layer, mate, col))

    for hop in range(1, 5):
        for kind in range(2):
            for way in range(2):
                if hop > limit[kind][way]:
                    continue
                place = praw.at[groups[kind], origin(way, hop)]
                remote(
                    place, place, send.at[kind, way, hop - 1], recv.at[kind, way, hop - 1],
                    layer, row, step_to[way],
                ).wait_recv()
                if hop < limit[kind][way]:
                    go(remote(
                        place, place, send.at[kind, way, hop], recv.at[kind, way, hop],
                        layer, row, step_to[way],
                    ))
                go(remote(
                    place, place, far.at[0, kind, way, hop - 1], far.at[1, kind, way, hop - 1],
                    layer, mate, col,
                ))

    def low_part(kind, source):
        return lraw.at[source, pl.ds(384 * kind, 384), :]

    for kind in range(2):
        for way in range(2):
            half = x_ref.at[0, pl.ds(256 + 384 * kind, 384), :]
            go(remote(
                half, low_part(kind, col), lo_send.at[kind, way, 0], lo_recv.at[kind, way, 0],
                layer, row, step_to[way],
            ))

    def low_hop(hop):
        for kind in range(2):
            for way in range(2):
                if hop > limit[kind][way]:
                    continue
                place = low_part(kind, origin(way, hop))
                remote(
                    place, place, lo_send.at[kind, way, hop - 1], lo_recv.at[kind, way, hop - 1],
                    layer, row, step_to[way],
                ).wait_recv()
                if hop < limit[kind][way]:
                    remote(
                        place, place, lo_send.at[kind, way, hop], lo_recv.at[kind, way, hop],
                        layer, row, step_to[way],
                    ).start()

    mates = (mate, rows_n - 1 - row)
    place = praw.at[mates[0], col]
    remote(place, place, near.at[2], near.at[3], layer, mate, col).wait_recv()
    place = praw.at[mates[1], col]
    remote(place, place, near.at[4], near.at[5], layer, mate, col).wait_recv()
    place = uraw.at[over]
    remote(place, place, up_send.at[0], up_recv.at[0], layer, over, col).wait_recv()
    go(remote(place, place, up_send.at[2], up_recv.at[2], layer, mate, col))
    for hop in range(1, 5):
        for kind in range(2):
            for way in range(2):
                if hop > limit[kind][way]:
                    continue
                place = praw.at[mates[kind], origin(way, hop)]
                remote(
                    place, place, far.at[0, kind, way, hop - 1], far.at[1, kind, way, hop - 1],
                    layer, mate, col,
                ).wait_recv()
    place = uraw.at[mates[0]]
    remote(place, place, up_send.at[1], up_recv.at[1], layer, mate, col).wait_recv()
    place = uraw.at[mates[1]]
    remote(place, place, up_send.at[2], up_recv.at[2], layer, mate, col).wait_recv()

    def filled(i, j):
        return mask_ref[i, j].astype(jnp.float32)

    @pl.loop(0, 8)
    def _(i):
        group, part = i // 2, pl.multiple_of(lax.rem(i, 2) * BS, BS)
        here = pl.ds(pl.multiple_of(i * BS, BS), BS)
        for j in range(8):
            work[here, j * BS : (j + 1) * BS] = praw[group, j, pl.ds(part, BS), :] * filled(i, j)
        for b in range(3):
            work[here, 1024 + b * BS : 1024 + (b + 1) * BS] = (
                uraw[group, b, pl.ds(part, BS), :] * filled(i, 8 * (b + 1) + col)
            )

    @pl.loop(0, 8)
    def _(j):
        here = pl.ds(pl.multiple_of(j * BS, BS), BS)
        inv[j] = invert(work[here, here], unit, scaled)
        for k in range(7):

            @pl.when(j == k)
            def _(k=k):
                begin, end = k * BS, (k + 1) * BS
                factors = bulk(work[end:1024, begin:end], inv[k])
                work[end:1024, begin:end] = factors
                for start in range(end, 1408, 256):
                    stop = min(start + 256, 1408)
                    work[end:1024, start:stop] -= bulk(factors, work[begin:end, start:stop])

        for hop in range(1, 5):

            @pl.when(j == 2 * hop - 1)
            def _(hop=hop):
                low_hop(hop)

    @pl.loop(0, 6)
    def _(i):
        here = pl.ds(pl.multiple_of(i * BS, BS), BS)
        block_row = 8 * (i // 2 + 1) + 2 * row + lax.rem(i, 2)
        for j in range(8):
            low[here, j * BS : (j + 1) * BS] = lraw[j, here, :] * filled(block_row, j)

    for k in range(8):
        begin, end = k * BS, (k + 1) * BS
        rest = low[:, begin:end]
        if k:
            rest = rest - bulk(low[:, :begin], work[:begin, begin:end])
        low[:, begin:end] = bulk(rest, inv[k])

    for a in range(3):
        here = slice(256 * a, 256 * a + 256)
        term = bulk(low[here, :], work[:, 1024:1408])
        for h in range(2):
            for b in range(3):
                block = x_ref[b + 1, 256 * (a + 1) + BS * h : 256 * (a + 1) + BS * (h + 1), :]
                block = block * filled(8 * (a + 1) + 2 * row + h, 8 * (b + 1) + col)
                block = block - term[BS * h : BS * (h + 1), BS * b : BS * (b + 1)]
                tail[a, BS * h : BS * (h + 1), BS * b : BS * (b + 1)] = block
        for d in range(1, layers):
            other = lax.rem(layer + d, layers)
            go(remote(
                tail.at[a, pl.ds(pl.multiple_of(other * 32, 32), 32), :], got.at[d, a],
                sum_send.at[d, a], sum_recv.at[d, a], other, row, col,
            ))

    mine, there = pl.ds(pl.multiple_of(row * 256, 256), 256), pl.ds(pl.multiple_of(col * BS, BS), BS)
    out_ref[pl.ds(0, 256, stride=4), :] = work[mine, there]
    for b in range(3):
        out_ref[pl.ds(b + 1, 256, stride=4), :] = work[mine, 1024 + BS * b : 1024 + BS * (b + 1)]
    for a in range(3):
        base = 1024 * (a + 1)
        out_ref[pl.ds(base, 256, stride=4), :] = low[256 * a : 256 * (a + 1), there]
        for b in range(3):
            out_ref[pl.ds(base + b + 1, 256, stride=4), :] = tail[a, :, BS * b : BS * (b + 1)]

    ours = pl.ds(pl.multiple_of(layer * 32, 32), 32)
    for a in range(3):
        for d in range(1, layers):
            place = got.at[d, a]
            remote(place, place, sum_send.at[d, a], sum_recv.at[d, a], layer, row, col).wait_recv()
        total = tail[a, ours, :]
        for d in range(1, layers):
            total = total + got[d, a]
        for b in range(3):
            anc_ref[pl.ds(96 * a + b, 32, stride=3), :] = total[:, BS * b : BS * (b + 1)]

    for copy in sent:
        copy.wait_send()
    for kind in range(2):
        for way in range(2):
            for hop in range(1, limit[kind][way]):
                place = low_part(kind, col)
                remote(
                    place, place, lo_send.at[kind, way, hop], lo_recv.at[kind, way, hop],
                    layer, row, step_to[way],
                ).wait_send()


def on_device(front_blocks, fill_mask):
    tiles = front_blocks[0].transpose(2, 0, 1, 3).reshape(4, 1024, 128)
    dma = pltpu.SemaphoreType.DMA
    vmem = lambda *shape: pltpu.VMEM(shape, jnp.float32)
    factored, ancestor = pl.pallas_call(
        kernel,
        out_shape=(
            jax.ShapeDtypeStruct((4096, 128), jnp.float32),
            jax.ShapeDtypeStruct((288, 128), jnp.float32),
        ),
        in_specs=[pl.BlockSpec(memory_space=pltpu.VMEM), pl.BlockSpec(memory_space=pltpu.SMEM)],
        out_specs=(pl.BlockSpec(memory_space=pltpu.VMEM), pl.BlockSpec(memory_space=pltpu.VMEM)),
        scratch_shapes=[
            vmem(4, 8, 256, 128), vmem(4, 3, 256, 128), vmem(8, 768, 128),
            vmem(1024, 1408), vmem(768, 1024), vmem(3, 256, 384), vmem(8, 3, 32, 384),
            vmem(8, 128, 128), vmem(128, 128), vmem(128, 128),
            dma((2, 2, 4)), dma((2, 2, 4)), dma((6,)), dma((2, 2, 2, 4)),
            dma((3,)), dma((3,)), dma((2, 2, 4)), dma((2, 2, 4)), dma((8, 3)), dma((8, 3)), dma((3,)),
        ],
        compiler_params=pltpu.CompilerParams(
            collective_id=0, has_side_effects=True, vmem_limit_bytes=60 * 1024 * 1024
        ),
        name="eliminate",
    )(tiles, fill_mask)
    return factored.reshape(1, 4, 256, 4, 128), ancestor.reshape(3, 1, 1, 32, 3, 128)


def solution(mesh):
    split = P("layer", None, "prow", None, "pcol")
    return jax.shard_map(
        on_device,
        mesh=mesh,
        in_specs=(split, P()),
        out_specs=(split, P(None, "prow", "layer", None, None, "pcol")),
        check_vma=False,
    )
```

time: 531 us -> 130 us (0.24); the launches traced: 524 us -> 130 us
  other arithmetic: 214 us -> 0 us
  Pallas kernels: 0 us -> 121 us
  local copies, waits for them, and re-layouts: 92.3 us -> 7.82 us
  matrix products: 77.4 us -> 0 us
  blocking collectives: 74.4 us -> 0 us
  waiting for transfers between devices: 39.9 us -> 0 us
  between operations: 15.5 us -> 0.64 us
  starting transfers between devices: 10.7 us -> 0 us
    another operation x41 -> x0, other arithmetic: 198 us -> none  [the longest x24 105 us: invert(): cholesky_factor = jnp.linalg.cholesky(gram_matrix)]
    pallas_call x0 -> x1, Pallas kernels: none -> 121 us  [on_device(): pl.pallas_call(kernel, out_shape=(jax.ShapeDtypeStruct((4096, 128), jnp.f...]
    all_gather x6 -> x0, blocking collectives: 74.4 us -> none  [all_blocks(): tiles = lax.all_gather(tiles, axes[k], axis=0, tiled=True)]
    dot_general x45 -> x0, matrix products: 67.3 us -> none  [full_dot(): jnp.dot(left, right, precision=lax.Precision.HIGHEST, preferred_element_t...]
    unnamed x134 -> x2, local copies, waits for them, and re-layouts: 52.4 us -> 3.72 us
    all_to_all x2 -> x0, waiting for transfers between devices: 31 us -> none  [the longest x1 17.9 us: sent_to_all(): return lax.all_to_all(copies, axis, split_axis=0, concat_axis=0, tiled=True)]
    all_to_all x2 -> x0, starting transfers between devices: 10.5 us -> none  [the longest x1 5.67 us: sent_to_all(): return lax.all_to_all(copies, axis, split_axis=0, concat_axis=0, tiled=True)]
    another operation x16 -> x0, matrix products: 10.1 us -> none  [invert(): return jax.scipy.linalg.cho_solve((cholesky_factor, True), pivot_tile.T)]
  transfers between devices with their start and end apart: 6 -> 0, of which waited for: 3 -> 0; matrix products, arithmetic and copies ran while one was open for 61% -> 0% of each run, Pallas kernels for 0% -> 0%
where the time goes in v1:
time: 130 us
  Pallas kernels  121 us (93%)
  local copies, waits for them, and re-layouts  7.82 us (6%)
    pallas_call x1, Pallas kernels, on_device(): pl.pallas_call(kernel, out_shape=(jax.ShapeDtypeStruct((4096, 128), jnp.f...  121 us
    unnamed x2, local copies, waits for them, and re-layouts  3.72 us
    transpose x1, local copies, waits for them, and re-layouts, on_device(): tiles = front_blocks[0].transpose(2, 0, 1, 3).reshape(4, 1024, 128)  3.14 us

profile of v1, /device:TPU:1, one launch (start us, length us, event | category | flops | bytes accessed | tf_op | source)
XLA Modules:
  0.0 129.6 jit_solution(2473759451087243106)
XLA Ops:
  0.6 3.1 %copy.6 = f32[4,4,256,128]{3,2,1,0:T(8,128)} copy(f32[4,4,256,128]{3,0,2,1:T(4,128)} %bitcast.6) | data formatting | bytes 4194304 | tf_op jit(solution)/shard_map/transpose | solution.py:298
  3.8 121.1 %eliminate.1 = (f32[4096,128]{1,0:T(8,128)}, f32[288,128]{1,0:T(8,128)}) custom-call(f32[4,1024,128]{2,1,0:T(8,128)} %bitcast.5, s32[32,32]{1,0:T(8,128)} %mask_ref.1), custom_call_target="tpu_custom_call" | custom-call | tf_op jit(solution)/shard_map/eliminate/pallas_call | solution.py:301
  124.9 1.0 reshape.15
  125.9 0.7 copy.7
  126.6 3.0 %copy.9 = f32[1,4,256,4,128]{4,3,2,1,0:T(4,128)} copy(f32[1,4,256,4,128]{4,3,2,1,0:T(4,128)} %bitcast.7) | data formatting | bytes 4194304

commit v2 on v1

--- a/solution.py
+++ b/solution.py
@@ -6,6 +6,7 @@
 from jax.sharding import PartitionSpec as P
 
 BS = 128
+LATE = 3
 MESH = pl.DeviceIdType.MESH
 
 
@@ -29,28 +30,45 @@
 
 def invert(pivot, unit_ref, scaled_ref):
     gram = dot(pivot, pivot, ((1,), (1,)))
-    groups = [gram[8 * p : 8 * p + 8, :] for p in range(BS // 8)]
+    count = BS // 8
+    half = count // 2
+    groups = [gram[8 * p : 8 * p + 8, :] for p in range(count)]
     lane = lax.broadcasted_iota(jnp.int32, (8, BS), 1)
     sub = lax.broadcasted_iota(jnp.int32, (8, BS), 0)
-    for p in range(BS // 8):
+    raw, done = [], []
+    for p in range(count):
+        if p == half:
+            term = dot(jnp.concatenate(raw, 0), jnp.concatenate(done, 0), ((0,), (0,)))
+            for q in range(half, count):
+                groups[q] = jnp.where(lane < 8 * half, 0.0, groups[q]) - term[8 * q : 8 * q + 8, :]
         rows = groups[p]
+        raw.append(rows)
         own = (lane >= 8 * p) & (lane < 8 * p + 8)
         eye = jnp.where(lane - 8 * p == sub, 1.0, 0.0)
         columns = [lanes_of(rows, 8 * p + j) for j in range(8)]
         unit_ref[8 * p : 8 * p + 8, :] = jnp.where(lane < 8 * p, rows, eye)
         rows = jnp.where(own, eye, rows)
-        for k in range(8):
-            at = sub == k
-            factor = columns[k]
-            scale = 1.0 / row_of(factor, k)
-            top = row_of(rows, k)
-            rows = jnp.where(at, top * scale, rows - (factor * top) * scale)
-            for j in range(k + 1, 8):
-                top = row_of(columns[j], k)
-                columns[j] = jnp.where(at, top * scale, columns[j] - (factor * top) * scale)
+        for k in range(0, 8, 2):
+            first, second = columns[k], columns[k + 1]
+            a, b = row_of(first, k), row_of(second, k)
+            c, d = row_of(first, k + 1), row_of(second, k + 1)
+            scale = 1.0 / (a * d - b * c)
+            at, after = sub == k, sub == k + 1
+            left = jnp.where(at, -d, jnp.where(after, c, first * d - second * c))
+            right = jnp.where(at, b, jnp.where(after, -a, second * a - first * b))
+
+            def cleared(block, k=k, pair=at | after, left=left, right=right, scale=scale):
+                term = left * row_of(block, k) + right * row_of(block, k + 1)
+                return jnp.where(pair, 0.0, block) - term * scale
+
+            rows = cleared(rows)
+            for j in range(k + 2, 8):
+                columns[j] = cleared(columns[j])
+        end = 8 * half if p < half else BS
+        done.append(jnp.where((lane < 8 * p + 8) | (lane >= end), rows, 0.0))
         scaled_ref[8 * p : 8 * p + 8, :] = jnp.where(lane < 8 * p + 8, rows, 0.0)
         tops = [row_of(rows, k) for k in range(8)]
-        for q in range(p + 1, BS // 8):
+        for q in range(p + 1, half if p < half else count):
             term = [lanes_of(groups[q], 8 * p + k) * tops[k] for k in range(8)]
             total = ((term[0] + term[1]) + (term[2] + term[3])) + ((term[4] + term[5]) + (term[6] + term[7]))
             groups[q] = jnp.where(own, 0.0, groups[q]) - total
@@ -58,9 +76,21 @@
     return dot(right, scaled_ref[...], ((0,), (0,)))
 
 
+def halves(value):
+    high = value.astype(jnp.bfloat16)
+    return high, (value - high.astype(jnp.float32)).astype(jnp.bfloat16)
+
+
+def passes(left, right):
+    def one(a, b):
+        return jnp.dot(a, b, preferred_element_type=jnp.float32)
+
+    return one(left[0], right[0]) + (one(left[0], right[1]) + one(left[1], right[0]))
+
+
 def kernel(
     x_ref, mask_ref, out_ref, anc_ref,
-    praw, uraw, lraw, work, low, tail, got, inv, unit, scaled,
+    praw, uraw, lraw, rest, work, low, low_high, low_low, up_high, up_low, pairs, tail, got, inv, unit, scaled,
     send, recv, near, far, up_send, up_recv, lo_send, lo_recv, sum_send, sum_recv, local,
 ):
     layer, row, col = lax.axis_index("layer"), lax.axis_index("prow"), lax.axis_index("pcol")
@@ -69,12 +99,16 @@
     over = lax.rem(row + 2, rows_n)
     right, left = lax.rem(col + 1, cols), lax.rem(col + cols - 1, cols)
 
-    own = [
-        pltpu.make_async_copy(x_ref.at[0, pl.ds(0, 256), :], praw.at[row, col], local.at[0]),
-        pltpu.make_async_copy(x_ref.at[0, pl.ds(256, 768), :], lraw.at[col], local.at[1]),
-        pltpu.make_async_copy(x_ref.at[pl.ds(1, 3), pl.ds(0, 256), :], uraw.at[row], local.at[2]),
+    own = [pltpu.make_async_copy(x_ref.at[0, :, 0, :], praw.at[row, col], local.at[0])]
+    for a in range(3):
+        own.append(pltpu.make_async_copy(x_ref.at[a + 1, :, 0, :], lraw.at[col, pl.ds(256 * a, 256), :], local.at[1 + a]))
+        own.append(pltpu.make_async_copy(x_ref.at[0, :, a + 1, :], uraw.at[row, a], local.at[4 + a]))
+    trailing = [
+        pltpu.make_async_copy(x_ref.at[a + 1, :, b + 1, :], rest.at[a, b], local.at[7 + 3 * a + b])
+        for a in range(3)
+        for b in range(3)
     ]
-    for copy in own:
+    for copy in own + trailing:
         copy.start()
 
     barrier = pltpu.get_barrier_semaphore()
@@ -90,6 +124,9 @@
         greet(lax.rem(layer + d, layers), row, col)
     pl.semaphore_wait(barrier, 4 + layers - 1)
 
+    for copy in own:
+        copy.wait()
+
     def remote(src, dst, send_sem, recv_sem, *device):
         return pltpu.make_async_remote_copy(
             src_ref=src, dst_ref=dst, send_sem=send_sem, recv_sem=recv_sem,
@@ -104,22 +141,18 @@
 
     groups = (row, over)
     limit = ((4, 3), (3, 4))
-    tile = x_ref.at[0, pl.ds(0, 256), :]
+    tile = praw.at[row, col]
     step_to = (right, left)
 
     def origin(way, hop):
         return lax.rem(col + (cols - hop if way == 0 else hop), cols)
 
-    go(remote(tile, praw.at[row, col], near.at[0], near.at[1], layer, over, col))
+    go(remote(tile, tile, near.at[0], near.at[1], layer, over, col))
     for way in range(2):
-        go(remote(tile, praw.at[row, col], send.at[0, way, 0], recv.at[0, way, 0], layer, row, step_to[way]))
-    go(remote(tile, praw.at[row, col], near.at[2], near.at[3], layer, mate, col))
-    blocks = x_ref.at[pl.ds(1, 3), pl.ds(0, 256), :]
-    go(remote(blocks, uraw.at[row], up_send.at[0], up_recv.at[0], layer, over, col))
-    go(remote(blocks, uraw.at[row], up_send.at[1], up_recv.at[1], layer, mate, col))
-    for copy in own:
-        copy.wait()
-
+        go(remote(tile, tile, send.at[0, way, 0], recv.at[0, way, 0], layer, row, step_to[way]))
+    go(remote(tile, tile, near.at[2], near.at[3], layer, mate, col))
+    blocks = uraw.at[row]
+    go(remote(blocks, blocks, up_send.at[0], up_recv.at[0], layer, over, col))
     place = praw.at[over, col]
     remote(place, place, near.at[0], near.at[1], layer, over, col).wait_recv()
     for way in range(2):
@@ -151,9 +184,9 @@
 
     for kind in range(2):
         for way in range(2):
-            half = x_ref.at[0, pl.ds(256 + 384 * kind, 384), :]
+            half = low_part(kind, col)
             go(remote(
-                half, low_part(kind, col), lo_send.at[kind, way, 0], lo_recv.at[kind, way, 0],
+                half, half, lo_send.at[kind, way, 0], lo_recv.at[kind, way, 0],
                 layer, row, step_to[way],
             ))
 
@@ -178,9 +211,7 @@
     remote(place, place, near.at[2], near.at[3], layer, mate, col).wait_recv()
     place = praw.at[mates[1], col]
     remote(place, place, near.at[4], near.at[5], layer, mate, col).wait_recv()
-    place = uraw.at[over]
-    remote(place, place, up_send.at[0], up_recv.at[0], layer, over, col).wait_recv()
-    go(remote(place, place, up_send.at[2], up_recv.at[2], layer, mate, col))
+    go(remote(blocks, blocks, up_send.at[1], up_recv.at[1], layer, mate, col))
     for hop in range(1, 5):
         for kind in range(2):
             for way in range(2):
@@ -191,10 +222,23 @@
                     place, place, far.at[0, kind, way, hop - 1], far.at[1, kind, way, hop - 1],
                     layer, mate, col,
                 ).wait_recv()
-    place = uraw.at[mates[0]]
-    remote(place, place, up_send.at[1], up_recv.at[1], layer, mate, col).wait_recv()
-    place = uraw.at[mates[1]]
-    remote(place, place, up_send.at[2], up_recv.at[2], layer, mate, col).wait_recv()
+    def up_over():
+        place = uraw.at[over]
+        remote(place, place, up_send.at[0], up_recv.at[0], layer, over, col).wait_recv()
+        remote(place, place, up_send.at[2], up_recv.at[2], layer, mate, col).start()
+
+    def up_here():
+        for k in range(2):
+            place = uraw.at[mates[k]]
+            remote(place, place, up_send.at[1 + k], up_recv.at[1 + k], layer, mate, col).wait_recv()
+        for i in range(8):
+            for b in range(3):
+                work[i * BS : (i + 1) * BS, 1024 + b * BS : 1024 + (b + 1) * BS] = (
+                    uraw[i // 2, b, (i % 2) * BS : (i % 2 + 1) * BS, :] * filled(i, 8 * (b + 1) + col)
+                )
+        for k in range(LATE):
+            begin, end = k * BS, (k + 1) * BS
+            work[end:1024, 1024:1408] -= bulk(work[end:1024, begin:end], work[begin:end, 1024:1408])
 
     def filled(i, j):
         return mask_ref[i, j].astype(jnp.float32)
@@ -205,15 +249,13 @@
         here = pl.ds(pl.multiple_of(i * BS, BS), BS)
         for j in range(8):
             work[here, j * BS : (j + 1) * BS] = praw[group, j, pl.ds(part, BS), :] * filled(i, j)
-        for b in range(3):
-            work[here, 1024 + b * BS : 1024 + (b + 1) * BS] = (
-                uraw[group, b, pl.ds(part, BS), :] * filled(i, 8 * (b + 1) + col)
-            )
 
     @pl.loop(0, 8)
     def _(j):
         here = pl.ds(pl.multiple_of(j * BS, BS), BS)
         inv[j] = invert(work[here, here], unit, scaled)
+        pl.when(j == 1)(up_over)
+        pl.when(j == LATE)(up_here)
         for k in range(7):
 
             @pl.when(j == k)
@@ -221,8 +263,9 @@
                 begin, end = k * BS, (k + 1) * BS
                 factors = bulk(work[end:1024, begin:end], inv[k])
                 work[end:1024, begin:end] = factors
-                for start in range(end, 1408, 256):
-                    stop = min(start + 256, 1408)
+                last = 1408 if k >= LATE else 1024
+                for start in range(end, last, 256):
+                    stop = min(start + 256, last)
                     work[end:1024, start:stop] -= bulk(factors, work[begin:end, start:stop])
 
         for hop in range(1, 5):
@@ -238,19 +281,36 @@
         for j in range(8):
             low[here, j * BS : (j + 1) * BS] = lraw[j, here, :] * filled(block_row, j)
 
-    for k in range(8):
-        begin, end = k * BS, (k + 1) * BS
-        rest = low[:, begin:end]
-        if k:
-            rest = rest - bulk(low[:, :begin], work[:begin, begin:end])
-        low[:, begin:end] = bulk(rest, inv[k])
-
+    for m in range(4):
+        first, second = inv[2 * m], inv[2 * m + 1]
+        between = work[256 * m : 256 * m + BS, 256 * m + BS : 256 * m + 256]
+        pairs[m, 0:BS, 0:BS] = first
+        pairs[m, BS:256, BS:256] = second
+        pairs[m, BS:256, 0:BS] = jnp.zeros((BS, BS), jnp.float32)
+        pairs[m, 0:BS, BS:256] = -bulk(first, bulk(between, second))
+    up_high[...], up_low[...] = halves(work[:, 1024:1408])
+
+    for m in range(4):
+        begin, end = 256 * m, 256 * m + 256
+        pair = halves(pairs[m])
+        above = halves(work[:begin, begin:end]) if m else None
+        for a in range(3):
+            here = slice(256 * a, 256 * a + 256)
+            value = low[here, begin:end]
+            if m:
+                value = value - passes((low_high[here, :begin], low_low[here, :begin]), above)
+            value = passes(halves(value), pair)
+            low[here, begin:end] = value
+            low_high[here, begin:end], low_low[here, begin:end] = halves(value)
+
+    for copy in trailing:
+        copy.wait()
     for a in range(3):
         here = slice(256 * a, 256 * a + 256)
-        term = bulk(low[here, :], work[:, 1024:1408])
+        term = passes((low_high[here, :], low_low[here, :]), (up_high[...], up_low[...]))
         for h in range(2):
             for b in range(3):
-                block = x_ref[b + 1, 256 * (a + 1) + BS * h : 256 * (a + 1) + BS * (h + 1), :]
+                block = rest[a, b, BS * h : BS * (h + 1), :]
                 block = block * filled(8 * (a + 1) + 2 * row + h, 8 * (b + 1) + col)
                 block = block - term[BS * h : BS * (h + 1), BS * b : BS * (b + 1)]
                 tail[a, BS * h : BS * (h + 1), BS * b : BS * (b + 1)] = block
@@ -280,10 +340,11 @@
         for d in range(1, layers):
             total = total + got[d, a]
         for b in range(3):
-            anc_ref[pl.ds(96 * a + b, 32, stride=3), :] = total[:, BS * b : BS * (b + 1)]
+            anc_ref[a, b] = total[:, BS * b : BS * (b + 1)]
 
     for copy in sent:
         copy.wait_send()
+    remote(blocks, blocks, up_send.at[2], up_recv.at[2], layer, mate, col).wait_send()
     for kind in range(2):
         for way in range(2):
             for hop in range(1, limit[kind][way]):
@@ -295,30 +356,31 @@
 
 
 def on_device(front_blocks, fill_mask):
-    tiles = front_blocks[0].transpose(2, 0, 1, 3).reshape(4, 1024, 128)
     dma = pltpu.SemaphoreType.DMA
     vmem = lambda *shape: pltpu.VMEM(shape, jnp.float32)
+    narrow = lambda *shape: pltpu.VMEM(shape, jnp.bfloat16)
     factored, ancestor = pl.pallas_call(
         kernel,
         out_shape=(
             jax.ShapeDtypeStruct((4096, 128), jnp.float32),
-            jax.ShapeDtypeStruct((288, 128), jnp.float32),
+            jax.ShapeDtypeStruct((3, 3, 32, 128), jnp.float32),
         ),
-        in_specs=[pl.BlockSpec(memory_space=pltpu.VMEM), pl.BlockSpec(memory_space=pltpu.SMEM)],
+        in_specs=[pl.BlockSpec(memory_space=pl.ANY), pl.BlockSpec(memory_space=pltpu.SMEM)],
         out_specs=(pl.BlockSpec(memory_space=pltpu.VMEM), pl.BlockSpec(memory_space=pltpu.VMEM)),
         scratch_shapes=[
             vmem(4, 8, 256, 128), vmem(4, 3, 256, 128), vmem(8, 768, 128),
-            vmem(1024, 1408), vmem(768, 1024), vmem(3, 256, 384), vmem(8, 3, 32, 384),
+            vmem(3, 3, 256, 128), vmem(1024, 1408), vmem(768, 1024), narrow(768, 1024), narrow(768, 1024),
+            narrow(1024, 384), narrow(1024, 384), vmem(4, 256, 256), vmem(3, 256, 384), vmem(8, 3, 32, 384),
             vmem(8, 128, 128), vmem(128, 128), vmem(128, 128),
             dma((2, 2, 4)), dma((2, 2, 4)), dma((6,)), dma((2, 2, 2, 4)),
-            dma((3,)), dma((3,)), dma((2, 2, 4)), dma((2, 2, 4)), dma((8, 3)), dma((8, 3)), dma((3,)),
+            dma((3,)), dma((3,)), dma((2, 2, 4)), dma((2, 2, 4)), dma((8, 3)), dma((8, 3)), dma((16,)),
         ],
         compiler_params=pltpu.CompilerParams(
             collective_id=0, has_side_effects=True, vmem_limit_bytes=60 * 1024 * 1024
         ),
         name="eliminate",
-    )(tiles, fill_mask)
-    return factored.reshape(1, 4, 256, 4, 128), ancestor.reshape(3, 1, 1, 32, 3, 128)
+    )(front_blocks[0], fill_mask)
+    return factored.reshape(1, 4, 256, 4, 128), ancestor.transpose(0, 2, 1, 3).reshape(3, 1, 1, 32, 3, 128)
 
 
 def solution(mesh):

time: 130 us -> 115 us (0.88)
  Pallas kernels: 121 us -> 110 us
  local copies, waits for them, and re-layouts: 7.82 us -> 3.75 us
    pallas_call x1, Pallas kernels: 121 us -> 110 us  [on_device(): pl.pallas_call(kernel, out_shape=(jax.ShapeDtypeStruct((4096, 128), jnp.f...]
    transpose x1 -> x0, local copies, waits for them, and re-layouts: 3.14 us -> none  [on_device(): tiles = front_blocks[0].transpose(2, 0, 1, 3).reshape(4, 1024, 128)]
    unnamed x2 -> x4, local copies, waits for them, and re-layouts: 3.72 us -> 3.75 us
where the time goes in v2:
time: 115 us
  Pallas kernels  110 us (96%)
  local copies, waits for them, and re-layouts  3.75 us (3%)
    pallas_call x1, Pallas kernels, on_device(): pl.pallas_call(kernel, out_shape=(jax.ShapeDtypeStruct((4096, 128), jnp.f...  110 us
    unnamed x4, local copies, waits for them, and re-layouts  3.75 us

profile of v2, /device:TPU:1, one launch (start us, length us, event | category | flops | bytes accessed | tf_op | source)
XLA Modules:
  0.0 114.9 jit_solution(1522868060557121049)
XLA Ops:
  0.6 110.5 %eliminate.1 = (f32[4096,128]{1,0:T(8,128)}, f32[3,3,32,128]{3,2,1,0:T(8,128)}) custom-call(f32[4,256,4,128]{3,2,1,0:T(4,128)} %bitcast.7, s32[32,32]{1,0:T(8,128)} %mask_ref.1), custom_call_target="tpu_custom_call" | custom-call | tf_op jit(solution)/shard_map/eliminate/pallas_call | solution.py:362
  111.1 0.0 copy-start
  111.1 3.1 %copy.7 = f32[1,4,256,4,128]{4,3,2,1,0:T(4,128)} copy(f32[1,4,256,4,128]{4,3,2,1,0:T(4,128)} %bitcast.8) | data formatting | bytes 4194304
  114.2 0.0 copy-done
  114.2 0.7 copy.8
Async XLA Ops:
  111.1 3.1 %copy-start = (f32[3,3,32,128]{3,2,1,0:T(8,128)S(1)}, f32[3,3,32,128]{3,2,1,0:T(8,128)}, u32[]{:S(2)}) copy-start(f32[3,3,32,128]{3,2,1,0:T(8,128)} %get-tuple-element.5) | copy-start | bytes 442372

commit v3 on v2

--- a/solution.py
+++ b/solution.py
@@ -6,8 +6,14 @@
 from jax.sharding import PartitionSpec as P
 
 BS = 128
-LATE = 3
+WIDE = 16
+SPAN = 32
+LATE = 1
 MESH = pl.DeviceIdType.MESH
+ORDER = (
+    (0, 0, 1), (0, 1, 1), (1, 0, 0), (0, 0, 2), (0, 1, 2), (1, 1, 0), (1, 0, 1), (0, 0, 3), (0, 1, 3), (1, 1, 1),
+    (1, 0, 2), (0, 0, 4), (0, 1, 4), (1, 1, 2), (1, 0, 3), (1, 1, 3), (1, 0, 4), (1, 1, 4),
+)
 
 
 def dot(left, right, dims=((1,), (0,)), precision=lax.Precision.HIGHEST):
@@ -21,34 +27,36 @@
 
 
 def lanes_of(block, column):
-    return jnp.broadcast_to(block[:, column : column + 1], (8, BS))
+    return jnp.broadcast_to(block[:, column : column + 1], (WIDE, BS))
 
 
 def row_of(block, row):
-    return jnp.broadcast_to(block[row : row + 1, :], (8, BS))
+    return jnp.broadcast_to(block[row : row + 1, :], (WIDE, BS))
 
 
 def invert(pivot, unit_ref, scaled_ref):
     gram = dot(pivot, pivot, ((1,), (1,)))
-    count = BS // 8
-    half = count // 2
-    groups = [gram[8 * p : 8 * p + 8, :] for p in range(count)]
-    lane = lax.broadcasted_iota(jnp.int32, (8, BS), 1)
-    sub = lax.broadcasted_iota(jnp.int32, (8, BS), 0)
+    count, span = BS // WIDE, SPAN // WIDE
+    groups = [gram[WIDE * p : WIDE * (p + 1), :] for p in range(count)]
+    lane = lax.broadcasted_iota(jnp.int32, (WIDE, BS), 1)
+    sub = lax.broadcasted_iota(jnp.int32, (WIDE, BS), 0)
     raw, done = [], []
     for p in range(count):
-        if p == half:
+        start, stop = WIDE * p, WIDE * (p + 1)
+        if p and p % span == 0:
             term = dot(jnp.concatenate(raw, 0), jnp.concatenate(done, 0), ((0,), (0,)))
-            for q in range(half, count):
-                groups[q] = jnp.where(lane < 8 * half, 0.0, groups[q]) - term[8 * q : 8 * q + 8, :]
+            raw, done = [], []
+            for q in range(p, count):
+                kept = jnp.where((lane >= start - SPAN) & (lane < start), 0.0, groups[q])
+                groups[q] = kept - term[WIDE * q : WIDE * (q + 1), :]
         rows = groups[p]
         raw.append(rows)
-        own = (lane >= 8 * p) & (lane < 8 * p + 8)
-        eye = jnp.where(lane - 8 * p == sub, 1.0, 0.0)
-        columns = [lanes_of(rows, 8 * p + j) for j in range(8)]
-        unit_ref[8 * p : 8 * p + 8, :] = jnp.where(lane < 8 * p, rows, eye)
+        own = (lane >= start) & (lane < stop)
+        eye = jnp.where(lane - start == sub, 1.0, 0.0)
+        columns = [lanes_of(rows, start + j) for j in range(WIDE)]
+        unit_ref[start:stop, :] = jnp.where(lane < start, rows, eye)
         rows = jnp.where(own, eye, rows)
-        for k in range(0, 8, 2):
+        for k in range(0, WIDE, 2):
             first, second = columns[k], columns[k + 1]
             a, b = row_of(first, k), row_of(second, k)
             c, d = row_of(first, k + 1), row_of(second, k + 1)
@@ -62,16 +70,17 @@
                 return jnp.where(pair, 0.0, block) - term * scale
 
             rows = cleared(rows)
-            for j in range(k + 2, 8):
+            for j in range(k + 2, WIDE):
                 columns[j] = cleared(columns[j])
-        end = 8 * half if p < half else BS
-        done.append(jnp.where((lane < 8 * p + 8) | (lane >= end), rows, 0.0))
-        scaled_ref[8 * p : 8 * p + 8, :] = jnp.where(lane < 8 * p + 8, rows, 0.0)
-        tops = [row_of(rows, k) for k in range(8)]
-        for q in range(p + 1, half if p < half else count):
-            term = [lanes_of(groups[q], 8 * p + k) * tops[k] for k in range(8)]
-            total = ((term[0] + term[1]) + (term[2] + term[3])) + ((term[4] + term[5]) + (term[6] + term[7]))
-            groups[q] = jnp.where(own, 0.0, groups[q]) - total
+        end = (p // span + 1) * span
+        done.append(jnp.where((lane < stop) | (lane >= WIDE * end), rows, 0.0))
+        scaled_ref[start:stop, :] = jnp.where(lane < stop, rows, 0.0)
+        tops = [row_of(rows, k) for k in range(WIDE)]
+        for q in range(p + 1, end):
+            terms = [lanes_of(groups[q], start + k) * tops[k] for k in range(WIDE)]
+            while len(terms) > 1:
+                terms = [terms[i] + terms[i + 1] for i in range(0, len(terms), 2)]
+            groups[q] = jnp.where(own, 0.0, groups[q]) - terms[0]
     right = dot(unit_ref[...], pivot)
     return dot(right, scaled_ref[...], ((0,), (0,)))
 
@@ -99,16 +108,18 @@
     over = lax.rem(row + 2, rows_n)
     right, left = lax.rem(col + 1, cols), lax.rem(col + cols - 1, cols)
 
-    own = [pltpu.make_async_copy(x_ref.at[0, :, 0, :], praw.at[row, col], local.at[0])]
+    first = pltpu.make_async_copy(x_ref.at[0, :, 0, :], praw.at[row, col], local.at[0])
+    ups, lows = [], []
     for a in range(3):
-        own.append(pltpu.make_async_copy(x_ref.at[a + 1, :, 0, :], lraw.at[col, pl.ds(256 * a, 256), :], local.at[1 + a]))
-        own.append(pltpu.make_async_copy(x_ref.at[0, :, a + 1, :], uraw.at[row, a], local.at[4 + a]))
+        ups.append(pltpu.make_async_copy(x_ref.at[0, :, a + 1, :], uraw.at[row, a], local.at[4 + a]))
+        lows.append(pltpu.make_async_copy(x_ref.at[a + 1, :, 0, :], lraw.at[col, pl.ds(256 * a, 256), :], local.at[1 + a]))
     trailing = [
         pltpu.make_async_copy(x_ref.at[a + 1, :, b + 1, :], rest.at[a, b], local.at[7 + 3 * a + b])
         for a in range(3)
         for b in range(3)
     ]
-    for copy in own + trailing:
+    first.start()
+    for copy in ups:
         copy.start()
 
     barrier = pltpu.get_barrier_semaphore()
@@ -124,8 +135,7 @@
         greet(lax.rem(layer + d, layers), row, col)
     pl.semaphore_wait(barrier, 4 + layers - 1)
 
-    for copy in own:
-        copy.wait()
+    first.wait()
 
     def remote(src, dst, send_sem, recv_sem, *device):
         return pltpu.make_async_remote_copy(
@@ -141,47 +151,66 @@
 
     groups = (row, over)
     limit = ((4, 3), (3, 4))
-    tile = praw.at[row, col]
     step_to = (right, left)
 
     def origin(way, hop):
         return lax.rem(col + (cols - hop if way == 0 else hop), cols)
 
-    go(remote(tile, tile, near.at[0], near.at[1], layer, over, col))
-    for way in range(2):
-        go(remote(tile, tile, send.at[0, way, 0], recv.at[0, way, 0], layer, row, step_to[way]))
-    go(remote(tile, tile, near.at[2], near.at[3], layer, mate, col))
+    def chunk_at(group, source, chunk):
+        return praw.at[group, source, pl.ds(BS * chunk, BS), :]
+
+    def ring(place, kind, chunk, way, hop):
+        return remote(
+            place, place, send.at[kind, chunk, way, hop], recv.at[kind, chunk, way, hop], layer, row, step_to[way]
+        )
+
+    def passed(place, kind, chunk, way, hop):
+        return remote(
+            place, place, far.at[0, kind, chunk, way, hop], far.at[1, kind, chunk, way, hop], layer, mate, col
+        )
+
+    def across(place, chunk):
+        return remote(place, place, near.at[0, chunk], near.at[1, chunk], layer, over, col)
+
+    def beside(place, kind, chunk):
+        return remote(place, place, near.at[2 + 2 * kind, chunk], near.at[3 + 2 * kind, chunk], layer, mate, col)
+
+    for chunk in range(2):
+        place = chunk_at(row, col, chunk)
+        go(across(place, chunk))
+        for way in range(2):
+            go(ring(place, 0, chunk, way, 0))
+    for copy in lows + trailing:
+        copy.start()
+    for chunk in range(2):
+        go(beside(chunk_at(row, col, chunk), 0, chunk))
+    for copy in ups:
+        copy.wait()
     blocks = uraw.at[row]
     go(remote(blocks, blocks, up_send.at[0], up_recv.at[0], layer, over, col))
-    place = praw.at[over, col]
-    remote(place, place, near.at[0], near.at[1], layer, over, col).wait_recv()
-    for way in range(2):
-        go(remote(place, place, send.at[1, way, 0], recv.at[1, way, 0], layer, row, step_to[way]))
-    go(remote(place, place, near.at[4], near.at[5], layer, mate, col))
-
-    for hop in range(1, 5):
-        for kind in range(2):
+
+    for kind, chunk, hop in ORDER:
+        if hop == 0:
+            place = chunk_at(over, col, chunk)
+            across(place, chunk).wait_recv()
             for way in range(2):
-                if hop > limit[kind][way]:
-                    continue
-                place = praw.at[groups[kind], origin(way, hop)]
-                remote(
-                    place, place, send.at[kind, way, hop - 1], recv.at[kind, way, hop - 1],
-                    layer, row, step_to[way],
-                ).wait_recv()
-                if hop < limit[kind][way]:
-                    go(remote(
-                        place, place, send.at[kind, way, hop], recv.at[kind, way, hop],
-                        layer, row, step_to[way],
-                    ))
-                go(remote(
-                    place, place, far.at[0, kind, way, hop - 1], far.at[1, kind, way, hop - 1],
-                    layer, mate, col,
-                ))
+                go(ring(place, 1, chunk, way, 0))
+            go(beside(place, 1, chunk))
+            continue
+        for way in range(2):
+            if hop > limit[chunk][way]:
+                continue
+            place = chunk_at(groups[kind], origin(way, hop), chunk)
+            ring(place, kind, chunk, way, hop - 1).wait_recv()
+            if hop < limit[chunk][way]:
+                go(ring(place, kind, chunk, way, hop))
+            go(passed(place, kind, chunk, way, hop - 1))
 
     def low_part(kind, source):
         return lraw.at[source, pl.ds(384 * kind, 384), :]
 
+    for copy in lows:
+        copy.wait()
     for kind in range(2):
         for way in range(2):
             half = low_part(kind, col)
@@ -190,38 +219,33 @@
                 layer, row, step_to[way],
             ))
 
-    def low_hop(hop):
-        for kind in range(2):
-            for way in range(2):
-                if hop > limit[kind][way]:
-                    continue
-                place = low_part(kind, origin(way, hop))
-                remote(
-                    place, place, lo_send.at[kind, way, hop - 1], lo_recv.at[kind, way, hop - 1],
-                    layer, row, step_to[way],
-                ).wait_recv()
-                if hop < limit[kind][way]:
-                    remote(
-                        place, place, lo_send.at[kind, way, hop], lo_recv.at[kind, way, hop],
-                        layer, row, step_to[way],
-                    ).start()
+    def low_ring(place, kind, way, hop):
+        return remote(
+            place, place, lo_send.at[kind, way, hop], lo_recv.at[kind, way, hop], layer, row, step_to[way]
+        )
+
+    def low_hop(kind, hop):
+        for way in range(2):
+            if hop > limit[kind][way]:
+                continue
+            place = low_part(kind, origin(way, hop))
+            low_ring(place, kind, way, hop - 1).wait_recv()
+            if hop < limit[kind][way]:
+                low_ring(place, kind, way, hop).start()
+
+    go(remote(blocks, blocks, up_send.at[1], up_recv.at[1], layer, mate, col))
 
     mates = (mate, rows_n - 1 - row)
-    place = praw.at[mates[0], col]
-    remote(place, place, near.at[2], near.at[3], layer, mate, col).wait_recv()
-    place = praw.at[mates[1], col]
-    remote(place, place, near.at[4], near.at[5], layer, mate, col).wait_recv()
-    go(remote(blocks, blocks, up_send.at[1], up_recv.at[1], layer, mate, col))
-    for hop in range(1, 5):
-        for kind in range(2):
-            for way in range(2):
-                if hop > limit[kind][way]:
-                    continue
-                place = praw.at[mates[kind], origin(way, hop)]
-                remote(
-                    place, place, far.at[0, kind, way, hop - 1], far.at[1, kind, way, hop - 1],
-                    layer, mate, col,
-                ).wait_recv()
+    for kind, chunk, hop in ORDER:
+        if hop == 0:
+            beside(chunk_at(mates[1], col, chunk), 1, chunk).wait_recv()
+            beside(chunk_at(mates[0], col, chunk), 0, chunk).wait_recv()
+            continue
+        for way in range(2):
+            if hop <= limit[chunk][way]:
+                place = chunk_at(mates[kind], origin(way, hop), chunk)
+                passed(place, kind, chunk, way, hop - 1).wait_recv()
+
     def up_over():
         place = uraw.at[over]
         remote(place, place, up_send.at[0], up_recv.at[0], layer, over, col).wait_recv()
@@ -254,7 +278,7 @@
     def _(j):
         here = pl.ds(pl.multiple_of(j * BS, BS), BS)
         inv[j] = invert(work[here, here], unit, scaled)
-        pl.when(j == 1)(up_over)
+        pl.when(j == 0)(up_over)
         pl.when(j == LATE)(up_here)
         for k in range(7):
 
@@ -269,10 +293,11 @@
                     work[end:1024, start:stop] -= bulk(factors, work[begin:end, start:stop])
 
         for hop in range(1, 5):
-
-            @pl.when(j == 2 * hop - 1)
-            def _(hop=hop):
-                low_hop(hop)
+            for kind in range(2):
+
+                @pl.when(j == 2 * hop - 2 + kind)
+                def _(kind=kind, hop=hop):
+                    low_hop(kind, hop)
 
     @pl.loop(0, 6)
     def _(i):
@@ -348,11 +373,18 @@
     for kind in range(2):
         for way in range(2):
             for hop in range(1, limit[kind][way]):
-                place = low_part(kind, col)
-                remote(
-                    place, place, lo_send.at[kind, way, hop], lo_recv.at[kind, way, hop],
-                    layer, row, step_to[way],
-                ).wait_send()
+                low_ring(low_part(kind, col), kind, way, hop).wait_send()
+
+
+def handed_on(staged_ref, out_ref, sems):
+    copies = [
+        pltpu.make_async_copy(staged_ref.at[pl.ds(1024 * k, 1024)], out_ref.at[pl.ds(1024 * k, 1024)], sems.at[k])
+        for k in range(4)
+    ]
+    for copy in copies:
+        copy.start()
+    for copy in copies:
+        copy.wait()
 
 
 def on_device(front_blocks, fill_mask):
@@ -362,7 +394,7 @@
     factored, ancestor = pl.pallas_call(
         kernel,
         out_shape=(
-            jax.ShapeDtypeStruct((4096, 128), jnp.float32),
+            pltpu.VMEM((4096, 128), jnp.float32),
             jax.ShapeDtypeStruct((3, 3, 32, 128), jnp.float32),
         ),
         in_specs=[pl.BlockSpec(memory_space=pl.ANY), pl.BlockSpec(memory_space=pltpu.SMEM)],
@@ -372,7 +404,7 @@
             vmem(3, 3, 256, 128), vmem(1024, 1408), vmem(768, 1024), narrow(768, 1024), narrow(768, 1024),
             narrow(1024, 384), narrow(1024, 384), vmem(4, 256, 256), vmem(3, 256, 384), vmem(8, 3, 32, 384),
             vmem(8, 128, 128), vmem(128, 128), vmem(128, 128),
-            dma((2, 2, 4)), dma((2, 2, 4)), dma((6,)), dma((2, 2, 2, 4)),
+            dma((2, 2, 2, 4)), dma((2, 2, 2, 4)), dma((6, 2)), dma((2, 2, 2, 2, 4)),
             dma((3,)), dma((3,)), dma((2, 2, 4)), dma((2, 2, 4)), dma((8, 3)), dma((8, 3)), dma((16,)),
         ],
         compiler_params=pltpu.CompilerParams(
@@ -380,6 +412,11 @@
         ),
         name="eliminate",
     )(front_blocks[0], fill_mask)
+    factored = pl.pallas_call(
+        handed_on, out_shape=jax.ShapeDtypeStruct((4096, 128), jnp.float32),
+        in_specs=[pl.BlockSpec(memory_space=pltpu.VMEM)], out_specs=pl.BlockSpec(memory_space=pl.ANY),
+        scratch_shapes=[dma((4,))], name="hand_on",
+    )(pltpu.with_memory_space_constraint(factored, pltpu.VMEM))
     return factored.reshape(1, 4, 256, 4, 128), ancestor.transpose(0, 2, 1, 3).reshape(3, 1, 1, 32, 3, 128)
 
 

time: 115 us -> 106 us (0.922)
  Pallas kernels: 110 us -> 105 us
  local copies, waits for them, and re-layouts: 3.75 us -> 0.67 us
    pallas_call x1 -> x2, Pallas kernels: 110 us -> 105 us  [the longest x1 104 us: on_device(): pl.pallas_call(kernel, out_shape=(pltpu.VMEM((4096, 128), jnp.float32), j...]
    unnamed x4 -> x3, local copies, waits for them, and re-layouts: 3.75 us -> 0.67 us
where the time goes in v3:
time: 106 us
  Pallas kernels  105 us (99%)
    pallas_call x1, Pallas kernels, on_device(): pl.pallas_call(kernel, out_shape=(pltpu.VMEM((4096, 128), jnp.float32), j...  104 us

profile of v3, /device:TPU:1, one launch (start us, length us, event | category | flops | bytes accessed | tf_op | source)
XLA Modules:
  0.0 106.3 jit_solution(156466321480149081)
XLA Ops:
  0.6 103.7 %eliminate.1 = (f32[4096,128]{1,0:T(8,128)S(1)}, f32[3,3,32,128]{3,2,1,0:T(8,128)}) custom-call(f32[4,256,4,128]{3,2,1,0:T(4,128)} %bitcast.7, s32[32,32]{1,0:T(8,128)} %mask_ref.1), custom_call_target="tpu_custom_call" | custom-call | tf_op jit(solution)/shard_map/eliminate/pallas_call | solution.py:394
  104.3 0.0 copy-start
  104.3 1.3 %hand_on.1 = f32[4096,128]{1,0:T(8,128)} custom-call(f32[4096,128]{1,0:T(8,128)S(1)} %get-tuple-element.4.staged_ref), custom_call_target="tpu_custom_call" | custom-call | tf_op jit(solution)/shard_map/hand_on/pallas_call | solution.py:415
  105.7 0.0 copy-done
  105.7 0.7 copy.6
Async XLA Ops:
  104.3 1.4 %copy-start = (f32[3,3,32,128]{3,2,1,0:T(8,128)S(1)}, f32[3,3,32,128]{3,2,1,0:T(8,128)}, u32[]{:S(2)}) copy-start(f32[3,3,32,128]{3,2,1,0:T(8,128)} %get-tuple-element.5) | copy-start | bytes 442372

commit v4 on v3

--- a/solution.py
+++ b/solution.py
@@ -293,18 +293,11 @@
                     work[end:1024, start:stop] -= bulk(factors, work[begin:end, start:stop])
 
         for hop in range(1, 5):
-            for kind in range(2):
+            for kind in range(2 if hop < 4 else 1):
 
                 @pl.when(j == 2 * hop - 2 + kind)
                 def _(kind=kind, hop=hop):
                     low_hop(kind, hop)
-
-    @pl.loop(0, 6)
-    def _(i):
-        here = pl.ds(pl.multiple_of(i * BS, BS), BS)
-        block_row = 8 * (i // 2 + 1) + 2 * row + lax.rem(i, 2)
-        for j in range(8):
-            low[here, j * BS : (j + 1) * BS] = lraw[j, here, :] * filled(block_row, j)
 
     for m in range(4):
         first, second = inv[2 * m], inv[2 * m + 1]
@@ -315,36 +308,45 @@
         pairs[m, 0:BS, BS:256] = -bulk(first, bulk(between, second))
     up_high[...], up_low[...] = halves(work[:, 1024:1408])
 
-    for m in range(4):
-        begin, end = 256 * m, 256 * m + 256
-        pair = halves(pairs[m])
-        above = halves(work[:begin, begin:end]) if m else None
-        for a in range(3):
+    def solve(supers):
+        for a in supers:
+            for h in range(2):
+                here = slice(256 * a + BS * h, 256 * a + BS * (h + 1))
+                for j in range(8):
+                    low[here, j * BS : (j + 1) * BS] = lraw[j, here, :] * filled(8 * (a + 1) + 2 * row + h, j)
+        for m in range(4):
+            begin, end = 256 * m, 256 * m + 256
+            pair = halves(pairs[m])
+            above = halves(work[:begin, begin:end]) if m else None
+            for a in supers:
+                here = slice(256 * a, 256 * a + 256)
+                value = low[here, begin:end]
+                if m:
+                    value = value - passes((low_high[here, :begin], low_low[here, :begin]), above)
+                value = passes(halves(value), pair)
+                low[here, begin:end] = value
+                low_high[here, begin:end], low_low[here, begin:end] = halves(value)
+        for a in supers:
             here = slice(256 * a, 256 * a + 256)
-            value = low[here, begin:end]
-            if m:
-                value = value - passes((low_high[here, :begin], low_low[here, :begin]), above)
-            value = passes(halves(value), pair)
-            low[here, begin:end] = value
-            low_high[here, begin:end], low_low[here, begin:end] = halves(value)
+            term = passes((low_high[here, :], low_low[here, :]), (up_high[...], up_low[...]))
+            for h in range(2):
+                for b in range(3):
+                    block = rest[a, b, BS * h : BS * (h + 1), :]
+                    block = block * filled(8 * (a + 1) + 2 * row + h, 8 * (b + 1) + col)
+                    block = block - term[BS * h : BS * (h + 1), BS * b : BS * (b + 1)]
+                    tail[a, BS * h : BS * (h + 1), BS * b : BS * (b + 1)] = block
+            for d in range(1, layers):
+                other = lax.rem(layer + d, layers)
+                go(remote(
+                    tail.at[a, pl.ds(pl.multiple_of(other * 32, 32), 32), :], got.at[d, a],
+                    sum_send.at[d, a], sum_recv.at[d, a], other, row, col,
+                ))
 
     for copy in trailing:
         copy.wait()
-    for a in range(3):
-        here = slice(256 * a, 256 * a + 256)
-        term = passes((low_high[here, :], low_low[here, :]), (up_high[...], up_low[...]))
-        for h in range(2):
-            for b in range(3):
-                block = rest[a, b, BS * h : BS * (h + 1), :]
-                block = block * filled(8 * (a + 1) + 2 * row + h, 8 * (b + 1) + col)
-                block = block - term[BS * h : BS * (h + 1), BS * b : BS * (b + 1)]
-                tail[a, BS * h : BS * (h + 1), BS * b : BS * (b + 1)] = block
-        for d in range(1, layers):
-            other = lax.rem(layer + d, layers)
-            go(remote(
-                tail.at[a, pl.ds(pl.multiple_of(other * 32, 32), 32), :], got.at[d, a],
-                sum_send.at[d, a], sum_recv.at[d, a], other, row, col,
-            ))
+    solve((0,))
+    low_hop(1, 4)
+    solve((1, 2))
 
     mine, there = pl.ds(pl.multiple_of(row * 256, 256), 256), pl.ds(pl.multiple_of(col * BS, BS), BS)
     out_ref[pl.ds(0, 256, stride=4), :] = work[mine, there]

time: 106 us -> 103 us (0.972)
  Pallas kernels: 105 us -> 102 us
    pallas_call x1, Pallas kernels: 104 us -> 101 us  [on_device(): pl.pallas_call(kernel, out_shape=(pltpu.VMEM((4096, 128), jnp.float32), j...]
where the time goes in v4:
time: 103 us
  Pallas kernels  102 us (99%)
    pallas_call x1, Pallas kernels, on_device(): pl.pallas_call(kernel, out_shape=(pltpu.VMEM((4096, 128), jnp.float32), j...  101 us

profile of v4, /device:TPU:1, one launch (start us, length us, event | category | flops | bytes accessed | tf_op | source)
XLA Modules:
  0.0 103.3 jit_solution(13380315025168754982)
XLA Ops:
  0.6 100.6 %eliminate.1 = (f32[4096,128]{1,0:T(8,128)S(1)}, f32[3,3,32,128]{3,2,1,0:T(8,128)}) custom-call(f32[4,256,4,128]{3,2,1,0:T(4,128)} %bitcast.7, s32[32,32]{1,0:T(8,128)} %mask_ref.1), custom_call_target="tpu_custom_call" | custom-call | tf_op jit(solution)/shard_map/eliminate/pallas_call | solution.py:396
  101.3 0.0 copy-start
  101.3 1.3 %hand_on.1 = f32[4096,128]{1,0:T(8,128)} custom-call(f32[4096,128]{1,0:T(8,128)S(1)} %get-tuple-element.4.staged_ref), custom_call_target="tpu_custom_call" | custom-call | tf_op jit(solution)/shard_map/hand_on/pallas_call | solution.py:417
  102.7 0.0 copy-done
  102.7 0.7 copy.6
Async XLA Ops:
  101.3 1.4 %copy-start = (f32[3,3,32,128]{3,2,1,0:T(8,128)S(1)}, f32[3,3,32,128]{3,2,1,0:T(8,128)}, u32[]{:S(2)}) copy-start(f32[3,3,32,128]{3,2,1,0:T(8,128)} %get-tuple-element.5) | copy-start | bytes 442372

commit v5 on v4

--- a/solution.py
+++ b/solution.py
@@ -169,8 +169,8 @@
             place, place, far.at[0, kind, chunk, way, hop], far.at[1, kind, chunk, way, hop], layer, mate, col
         )
 
-    def across(place, chunk):
-        return remote(place, place, near.at[0, chunk], near.at[1, chunk], layer, over, col)
+    def across(place, chunk, way=0):
+        return remote(place, place, near.at[way, chunk], near.at[way + 1, chunk], layer, over, col)
 
     def beside(place, kind, chunk):
         return remote(place, place, near.at[2 + 2 * kind, chunk], near.at[3 + 2 * kind, chunk], layer, mate, col)
@@ -186,8 +186,13 @@
         go(beside(chunk_at(row, col, chunk), 0, chunk))
     for copy in ups:
         copy.wait()
-    blocks = uraw.at[row]
-    go(remote(blocks, blocks, up_send.at[0], up_recv.at[0], layer, over, col))
+
+    def up_copy(block, way, group, *device):
+        place = uraw.at[group, block]
+        return remote(place, place, up_send.at[way, block], up_recv.at[way, block], *device)
+
+    for block in range(2):
+        go(up_copy(block, 0, row, layer, over, col))
 
     for kind, chunk, hop in ORDER:
         if hop == 0:
@@ -201,9 +206,16 @@
             if hop > limit[chunk][way]:
                 continue
             place = chunk_at(groups[kind], origin(way, hop), chunk)
-            ring(place, kind, chunk, way, hop - 1).wait_recv()
-            if hop < limit[chunk][way]:
+            if kind == 1 and hop == 4:
+                across(place, chunk, 6).wait_recv()
+            else:
+                ring(place, kind, chunk, way, hop - 1).wait_recv()
+            if hop < (limit[chunk][way], 3)[kind]:
                 go(ring(place, kind, chunk, way, hop))
+            if kind == 0 and hop == 4:
+                go(across(place, chunk, 6))
+                if chunk == 1:
+                    go(up_copy(2, 0, row, layer, over, col))
             go(passed(place, kind, chunk, way, hop - 1))
 
     def low_part(kind, source):
@@ -233,7 +245,8 @@
             if hop < limit[kind][way]:
                 low_ring(place, kind, way, hop).start()
 
-    go(remote(blocks, blocks, up_send.at[1], up_recv.at[1], layer, mate, col))
+    for block in range(3):
+        go(up_copy(block, 1, row, layer, mate, col))
 
     mates = (mate, rows_n - 1 - row)
     for kind, chunk, hop in ORDER:
@@ -247,14 +260,14 @@
                 passed(place, kind, chunk, way, hop - 1).wait_recv()
 
     def up_over():
-        place = uraw.at[over]
-        remote(place, place, up_send.at[0], up_recv.at[0], layer, over, col).wait_recv()
-        remote(place, place, up_send.at[2], up_recv.at[2], layer, mate, col).start()
+        for block in range(3):
+            up_copy(block, 0, over, layer, over, col).wait_recv()
+            up_copy(block, 2, over, layer, mate, col).start()
 
     def up_here():
-        for k in range(2):
-            place = uraw.at[mates[k]]
-            remote(place, place, up_send.at[1 + k], up_recv.at[1 + k], layer, mate, col).wait_recv()
+        for block in range(3):
+            for k in range(2):
+                up_copy(block, 1 + k, mates[k], layer, mate, col).wait_recv()
         for i in range(8):
             for b in range(3):
                 work[i * BS : (i + 1) * BS, 1024 + b * BS : 1024 + (b + 1) * BS] = (
@@ -371,7 +384,8 @@
 
     for copy in sent:
         copy.wait_send()
-    remote(blocks, blocks, up_send.at[2], up_recv.at[2], layer, mate, col).wait_send()
+    for block in range(3):
+        up_copy(block, 2, over, layer, mate, col).wait_send()
     for kind in range(2):
         for way in range(2):
             for hop in range(1, limit[kind][way]):
@@ -406,8 +420,8 @@
             vmem(3, 3, 256, 128), vmem(1024, 1408), vmem(768, 1024), narrow(768, 1024), narrow(768, 1024),
             narrow(1024, 384), narrow(1024, 384), vmem(4, 256, 256), vmem(3, 256, 384), vmem(8, 3, 32, 384),
             vmem(8, 128, 128), vmem(128, 128), vmem(128, 128),
-            dma((2, 2, 2, 4)), dma((2, 2, 2, 4)), dma((6, 2)), dma((2, 2, 2, 2, 4)),
-            dma((3,)), dma((3,)), dma((2, 2, 4)), dma((2, 2, 4)), dma((8, 3)), dma((8, 3)), dma((16,)),
+            dma((2, 2, 2, 4)), dma((2, 2, 2, 4)), dma((8, 2)), dma((2, 2, 2, 2, 4)),
+            dma((3, 3)), dma((3, 3)), dma((2, 2, 4)), dma((2, 2, 4)), dma((8, 3)), dma((8, 3)), dma((16,)),
         ],
         compiler_params=pltpu.CompilerParams(
             collective_id=0, has_side_effects=True, vmem_limit_bytes=60 * 1024 * 1024

time: 103 us -> 100 us (0.971)
  Pallas kernels: 102 us -> 98.8 us
    pallas_call x1, Pallas kernels: 101 us -> 97.5 us  [on_device(): pl.pallas_call(kernel, out_shape=(pltpu.VMEM((4096, 128), jnp.float32), j...]
where the time goes in v5:
time: 100 us
  Pallas kernels  98.8 us (99%)
    pallas_call x1, Pallas kernels, on_device(): pl.pallas_call(kernel, out_shape=(pltpu.VMEM((4096, 128), jnp.float32), j...  97.5 us

profile of v5, /device:TPU:1, one launch (start us, length us, event | category | flops | bytes accessed | tf_op | source)
XLA Modules:
  0.0 100.2 jit_solution(7170752819443138886)
XLA Ops:
  0.6 97.5 %eliminate.1 = (f32[4096,128]{1,0:T(8,128)S(1)}, f32[3,3,32,128]{3,2,1,0:T(8,128)}) custom-call(f32[4,256,4,128]{3,2,1,0:T(4,128)} %bitcast.7, s32[32,32]{1,0:T(8,128)} %mask_ref.1), custom_call_target="tpu_custom_call" | custom-call | tf_op jit(solution)/shard_map/eliminate/pallas_call | solution.py:410
  98.1 0.0 copy-start
  98.1 1.3 %hand_on.1 = f32[4096,128]{1,0:T(8,128)} custom-call(f32[4096,128]{1,0:T(8,128)S(1)} %get-tuple-element.4.staged_ref), custom_call_target="tpu_custom_call" | custom-call | tf_op jit(solution)/shard_map/hand_on/pallas_call | solution.py:431
  99.5 0.0 copy-done
  99.5 0.7 copy.6
Async XLA Ops:
  98.1 1.4 %copy-start = (f32[3,3,32,128]{3,2,1,0:T(8,128)S(1)}, f32[3,3,32,128]{3,2,1,0:T(8,128)}, u32[]{:S(2)}) copy-start(f32[3,3,32,128]{3,2,1,0:T(8,128)} %get-tuple-element.5) | copy-start | bytes 442372

commit v6 on v5

--- a/solution.py
+++ b/solution.py
@@ -348,7 +348,7 @@
                     block = block * filled(8 * (a + 1) + 2 * row + h, 8 * (b + 1) + col)
                     block = block - term[BS * h : BS * (h + 1), BS * b : BS * (b + 1)]
                     tail[a, BS * h : BS * (h + 1), BS * b : BS * (b + 1)] = block
-            for d in range(1, layers):
+            for d in (4, 3, 5, 2, 6, 1, 7):
                 other = lax.rem(layer + d, layers)
                 go(remote(
                     tail.at[a, pl.ds(pl.multiple_of(other * 32, 32), 32), :], got.at[d, a],
@@ -359,7 +359,8 @@
         copy.wait()
     solve((0,))
     low_hop(1, 4)
-    solve((1, 2))
+    solve((1,))
+    solve((2,))
 
     mine, there = pl.ds(pl.multiple_of(row * 256, 256), 256), pl.ds(pl.multiple_of(col * BS, BS), BS)
     out_ref[pl.ds(0, 256, stride=4), :] = work[mine, there]

time: 100 us -> 99.5 us (level)
  no operation moved by 1% of the time
where the time goes in v6:
time: 99.5 us; the launch traced here: 99.3 us
  Pallas kernels  98 us (98%)
    pallas_call x1, Pallas kernels, on_device(): pl.pallas_call(kernel, out_shape=(pltpu.VMEM((4096, 128), jnp.float32), j...  96.6 us

profile of v6, /device:TPU:1, one launch (start us, length us, event | category | flops | bytes accessed | tf_op | source)
XLA Modules:
  0.0 99.3 jit_solution(4860966410537668092)
XLA Ops:
  0.6 96.6 %eliminate.1 = (f32[4096,128]{1,0:T(8,128)S(1)}, f32[3,3,32,128]{3,2,1,0:T(8,128)}) custom-call(f32[4,256,4,128]{3,2,1,0:T(4,128)} %bitcast.7, s32[32,32]{1,0:T(8,128)} %mask_ref.1), custom_call_target="tpu_custom_call" | custom-call | tf_op jit(solution)/shard_map/eliminate/pallas_call | solution.py:411
  97.3 0.0 copy-start
  97.3 1.3 %hand_on.1 = f32[4096,128]{1,0:T(8,128)} custom-call(f32[4096,128]{1,0:T(8,128)S(1)} %get-tuple-element.4.staged_ref), custom_call_target="tpu_custom_call" | custom-call | tf_op jit(solution)/shard_map/hand_on/pallas_call | solution.py:432
  98.6 0.0 copy-done
  98.6 0.7 copy.6
Async XLA Ops:
  97.3 1.4 %copy-start = (f32[3,3,32,128]{3,2,1,0:T(8,128)S(1)}, f32[3,3,32,128]{3,2,1,0:T(8,128)}, u32[]{:S(2)}) copy-start(f32[3,3,32,128]{3,2,1,0:T(8,128)} %get-tuple-element.5) | copy-start | bytes 442372
